TPU v7x, 32 devices: a whole 2x2x4 slice. The times are simulated.
32 devices in a mesh: img: 2 (over x), sub: 16 (over z, y, core).
Axes of the slice: x: 2, y: 2, z: 4, core: 2. Of those that a mesh axis runs over, the one named last changes fastest.
Arguments:
- sub_images: float32 [2, 512, 4096], P(None, ('img', 'sub')), parts along dimension 1, may hold values from -6 to 6
- shift_table: int32 [4, 16, 2, 8], P(None, 'sub'), may hold values from -256 to 256
- phase_table: float32 [4, 16, 2, 8], P(None, 'sub'), may hold values from -3.140625 to 3.140625
- offset_table: int32 [4, 16, 2, 16], P(None, 'sub'), may hold values from 0 to 4
- weight_table: float32 [4, 16, 2, 4, 16], P(None, 'sub'), may hold values from -2 to 2
Outputs:
- turned_image: float32 [2, 8192, 256], P(None, ('img', 'sub')), parts along dimension 1
There are 2 independent parts, one for each index of `img`. A program takes and returns all parts, laid end to end along the dimension named above; an argument that names none is the same for every part. Nothing has to cross between parts.
All inputs are finite; a program needn't handle non-finite values.
Results may differ from a plain program's by a relative error of at most 0.0003.
Values sent between devices are 32-bit elements; how exact they have to be, the bound alone decides.
No kernel may reach another device: no remote copies, remote signals or barrier semaphores. Data moves between devices by JAX's collectives and lax.ppermute only.
A program may use at most 64 MiB of HBM per device.

v0:
```python
import functools
import math

import jax
import jax.numpy as jnp
import numpy as np
from jax import lax
from jax.experimental import pallas as pl
from jax.experimental.pallas import tpu as pltpu
from jax.sharding import PartitionSpec as P


LANES = 128
MXU = 256
CHUNK = 256
VMEM_GRANT = 12 << 20
f32 = jnp.float32
bf16 = jnp.bfloat16


def swapped(block, axis, stride):
    count = lax.axis_size(axis)
    route = []
    for low in range(count):
        high = low | 1 << stride
        if high != low and high < count:
            route += [(low, high), (high, low)]
    return lax.ppermute(block, axis, route)


def call(kernel, outs, ins, scratch, flops, after=(), space=pltpu.VMEM):
    moved = sum(math.prod(o.shape) * o.dtype.itemsize for o in outs)
    moved += sum(math.prod(i.shape) * i.dtype.itemsize for i in ins)
    count = len(ins)

    def run(*refs):
        kernel(*refs[:count], *refs[count + len(after) :])

    return pl.pallas_call(
        run,
        out_shape=outs,
        in_specs=[pl.BlockSpec(memory_space=space)] * count
        + [pl.BlockSpec(memory_space=pl.ANY)] * len(after),
        out_specs=[pl.BlockSpec(memory_space=pltpu.VMEM)] * len(outs),
        scratch_shapes=scratch,
        cost_estimate=pl.CostEstimate(flops=flops, bytes_accessed=moved, transcendentals=0),
        compiler_params=pltpu.CompilerParams(vmem_limit_bytes=VMEM_GRANT),
    )(*ins, *after)


def lane_matrix(direction, scale):
    k = np.arange(LANES)
    angle = direction * 2.0 * np.pi * (np.outer(k, k) % LANES) / LANES
    c, s = np.cos(angle) * scale, np.sin(angle) * scale
    full = np.block([[c, s], [-s, c]]).astype(np.float32)
    high = full.astype(bf16)
    low = (full - high.astype(np.float32)).astype(bf16)
    return high, low


def lane_twiddle(outer, direction):
    total = outer * LANES
    turns = np.outer(np.arange(outer), np.arange(LANES)) % total
    angle = direction * 2.0 * np.pi * turns / total
    return np.stack([np.cos(angle), np.sin(angle)]).astype(np.float32)


def times_constant(value, turn):
    real, imag = value
    turn = turn % 1.0
    if turn == 0.0:
        return value
    if turn == 0.5:
        return (-real, -imag)
    if turn == 0.25:
        return (-imag, real)
    if turn == 0.75:
        return (imag, -real)
    c, s = math.cos(2 * math.pi * turn), math.sin(2 * math.pi * turn)
    if abs(abs(c) - abs(s)) < 1e-12:
        r = abs(c)
        sc, ss = math.copysign(1, c), math.copysign(1, s)
        a = (real if sc > 0 else -real) - (imag if ss > 0 else -imag)
        b = (real if ss > 0 else -real) + (imag if sc > 0 else -imag)
        return (a * r, b * r)
    return (real * c - imag * s, real * s + imag * c)


def small_dft(values, direction):
    count = len(values)
    if count == 1:
        return values
    even = small_dft(values[0::2], direction)
    odd = small_dft(values[1::2], direction)
    first, second = [], []
    for k in range(count // 2):
        o = times_constant(odd[k], direction * k / count)
        e = even[k]
        first.append((e[0] + o[0], e[1] + o[1]))
        second.append((e[0] - o[0], e[1] - o[1]))
    return first + second


def split_factors(count):
    inner = 1 << ((count.bit_length() - 1) + 1) // 2
    return count // inner, inner


def staged_dft(count, direction, load, store, scratch):
    outer, inner = split_factors(count)
    for b in range(inner):
        got = small_dft([load(inner * a + b) for a in range(outer)], direction)
        for c in range(outer):
            value = times_constant(got[c], direction * b * c / count)
            scratch[0, c * inner + b] = value[0]
            scratch[1, c * inner + b] = value[1]
    for c in range(outer):
        line = [(scratch[0, c * inner + b], scratch[1, c * inner + b]) for b in range(inner)]
        got = small_dft(line, direction)
        for d in range(inner):
            store(c + outer * d, got[d])


def put_split(high_ref, low_ref, row, rows, value):
    for part in range(2):
        high = value[part].astype(bf16)
        low = (value[part] - high.astype(f32)).astype(bf16)
        high_ref[row : row + rows, part * LANES : (part + 1) * LANES] = high
        low_ref[row : row + rows, part * LANES : (part + 1) * LANES] = low


def dot3(left_high, left_low, right_high, right_low):
    def one(a, b):
        return jnp.dot(a, b, preferred_element_type=f32)

    return one(left_high, right_high) + (one(left_low, right_high) + one(left_high, right_low))


def put_halves(keep_ref, send_ref, bit, group, i, block, half):
    low, high = block[:half], block[half:]
    keep = jnp.where(bit == 0, low, high)
    send = jnp.where(bit == 0, high, low)
    for part in range(2):
        cut = slice(part * LANES, (part + 1) * LANES)
        keep_ref[part * group + i] = keep[:, cut]
        send_ref[part * group + i] = send[:, cut]


def cos_sin(turns, full):
    quarter = full // 4
    turns = turns & (full - 1)
    quadrant = (turns + quarter // 2) >> (quarter.bit_length() - 1)
    x = (turns - quadrant * quarter).astype(f32) * (2.0 * math.pi / full)
    y = x * x
    sine, cosine = 0.0, 0.0
    for term in (9, 7, 5, 3, 1):
        sine = sine * y + (-1.0) ** (term // 2) / math.factorial(term)
    for term in (10, 8, 6, 4, 2, 0):
        cosine = cosine * y + (-1.0) ** (term // 2) / math.factorial(term)
    sine = sine * x
    odd = (quadrant & 1) == 1
    first = jnp.where(odd, sine, cosine)
    second = jnp.where(odd, cosine, sine)
    first = jnp.where(((quadrant + 1) & 2) == 2, -first, first)
    return first, jnp.where((quadrant & 2) == 2, -second, second)


class Sizes:
    def __init__(self, rows, outer, taps, sub_count):
        self.rows, self.outer, self.taps, self.sub_count = rows, outer, taps, sub_count
        self.half = rows // 2
        self.levels = sub_count.bit_length() - 1
        self.last = self.levels - 1
        self.group = max(1, min(outer, CHUNK // rows))
        self.at_offset = 2 * taps
        self.at_shift = self.at_offset + 2
        self.at_phase = self.at_shift + 2
        self.record = -(-(self.at_phase + 2) // 8) * 8
        self.pages = -(-self.levels * self.record // LANES)
        self.slots = LANES // rows
        self.blocks = -(-sub_count // self.slots)
        self.chunks = outer // self.group
        self.last_page = self.last * self.record // LANES


def prepare(z, shift, phase, offset, weight, tabs, pack, lines):
    me = lax.axis_index("sub")
    lines[...] = jnp.zeros_like(lines)
    for level in range(z.levels):
        at = level * z.record
        for c in range(2):
            lines[at + c * z.taps : at + (c + 1) * z.taps, : z.rows] = weight[level, 0, c]
        at += z.at_offset
        lines[at : at + 2, : z.rows] = offset[level, 0].astype(f32)
        lines[at + 2 : at + 4, : z.half] = shift[level, 0].astype(f32)
        lines[at + 4 : at + 6, : z.half] = phase[level, 0]
    for page in range(z.pages):
        turned = lines[page * LANES : (page + 1) * LANES, :].T[: z.rows]
        tabs[:, page * LANES : (page + 1) * LANES] = turned
        if page == z.last_page:
            pack[: z.rows] = turned
    spread = lines[z.last * z.record : (z.last + 1) * z.record, :]
    step = z.rows
    while step < LANES:
        spread = spread + pltpu.roll(spread, step, 1)
        step *= 2
    slot = lax.broadcasted_iota(jnp.int32, spread.shape, 1) // z.rows
    for block in range(z.blocks):
        at = z.rows + block * z.record
        pack[at : at + z.record] = jnp.where(slot + block * z.slots == me, spread, 0.0)


def rotation(z, shifts, phases, near, far):
    full = 4 * z.outer * LANES
    shape = (z.rows, LANES)
    lane = lax.broadcasted_iota(jnp.int32, shape, 1)
    signed = z.outer * jnp.where(lane >= LANES // 2, lane - LANES, lane)
    shifts = jnp.broadcast_to(jnp.concatenate(shifts, axis=0), shape).astype(jnp.int32)
    phases = jnp.broadcast_to(jnp.concatenate(phases, axis=0), shape)
    c, s = cos_sin(shifts * signed, full)
    pc, ps = jnp.cos(phases), jnp.sin(phases)
    near[0] = pc * c + ps * s
    near[1] = ps * c - pc * s
    c, s = cos_sin(shifts * lane, full)
    far[0] = c
    far[1] = -s


def of_children(z, table, at):
    return [table[: z.half, at + c : at + c + 1] for c in range(2)]


def last_tables_kernel(z, pack, other, near, far):
    low = (lax.axis_index("sub") >> z.last & 1) == 0
    at = z.last * z.record - z.last_page * LANES
    both = []
    for row in (z.at_shift, z.at_phase):
        mine = of_children(z, pack, at + row)[0]
        their = of_children(z, other, at + row)[1]
        both.append([jnp.where(low, mine, their), jnp.where(low, their, mine)])
    rotation(z, *both, near, far)


def tables_kernel(z, tabs, near, far, wide_high, wide_low):
    for level in range(z.last):
        at = level * z.record
        shifts, phases = of_children(z, tabs, at + z.at_shift), of_children(z, tabs, at + z.at_phase)
        rotation(z, shifts, phases, near.at[level], far.at[level])
    size = z.group * z.rows
    shape = (z.rows, size)
    column = lax.broadcasted_iota(jnp.int32, shape, 1)
    beam = column % z.half
    child = (column // z.half) % 2
    block = column // z.rows
    for level in range(z.last):
        at = level * z.record
        wide = jnp.zeros(shape, f32)
        for c in range(2):
            first = tabs[:, at + z.at_offset + c : at + z.at_offset + c + 1].astype(jnp.int32)
            for tap in range(z.taps):
                hits = (beam == first + tap) & (child == c)
                wide += jnp.where(hits, tabs[:, at + c * z.taps + tap : at + c * z.taps + tap + 1], 0.0)
        for i in range(z.group):
            value = jnp.where(block == i, wide, 0.0)
            high = value.astype(bf16)
            wide_high[level, i * z.rows : (i + 1) * z.rows] = high
            wide_low[level, i * z.rows : (i + 1) * z.rows] = (value - high.astype(f32)).astype(bf16)


def last_blend_kernel(z, ours, theirs, blend_high, blend_low):
    tail = z.blocks * z.record
    known = ours[ours.shape[0] - tail :] + theirs[theirs.shape[0] - tail :]
    me = lax.axis_index("sub")
    beams = z.sub_count * z.rows
    for block in range(beams // LANES):
        table = known[block * z.record : (block + 1) * z.record]
        shape = (z.rows, LANES)
        row = lax.broadcasted_iota(jnp.int32, shape, 0)
        owner = lax.broadcasted_iota(jnp.int32, shape, 1) // z.rows + block * z.slots
        mine = (row // z.half) == (owner >> z.last & 1)
        parts = []
        for c in range(2):
            first = jnp.broadcast_to(table[z.at_offset + c : z.at_offset + c + 1].astype(jnp.int32), shape)
            total = jnp.zeros(shape, f32)
            for tap in range(z.taps):
                hits = (row % z.half == first + tap) & mine
                line = jnp.broadcast_to(table[c * z.taps + tap : c * z.taps + tap + 1], shape)
                total += jnp.where(hits, line, 0.0)
            parts.append(total)
        for away in range(z.sub_count):
            source = me ^ away
            value = jnp.where(owner == source, parts[0], 0.0)
            value = jnp.where(owner == (source ^ (1 << z.last)), parts[1], value)
            high = value.astype(bf16)
            at = (slice(away * z.rows, (away + 1) * z.rows), slice(block * LANES, (block + 1) * LANES))
            blend_high[at] = high
            blend_low[at] = (value - high.astype(f32)).astype(bf16)


def start_kernel(z, *refs):
    sources, refs = refs[:8], refs[8:]
    tabs, pack, refs = refs[0], refs[1], refs[2:]
    keeps, sends, refs = refs[: z.chunks], refs[z.chunks : 2 * z.chunks], refs[2 * z.chunks :]
    held, (lines, mid, high, low, sems) = refs[:8], refs[8:]
    copies = [
        pltpu.make_async_copy(source, place, sems.at[i])
        for i, (source, place) in enumerate(zip(sources, held))
    ]
    for copy in copies:
        copy.start()
    for copy in copies[:4]:
        copy.wait()
    prepare(z, *held[:4], tabs, pack, lines)
    image, twiddle, high_m, low_m = held[4:]
    copies[4].wait()
    copies[5].wait()

    def load(q):
        cut = slice(q * LANES, (q + 1) * LANES)
        return image[0, :, cut], image[1, :, cut]

    def store(k, value):
        c, s = twiddle[0, k : k + 1, :], twiddle[1, k : k + 1, :]
        value = (value[0] * c - value[1] * s, value[0] * s + value[1] * c)
        put_split(high, low, k * z.rows, z.rows, value)

    staged_dft(z.outer, -1, load, store, mid)
    bit = lax.axis_index("sub") & 1
    size = z.group * z.rows
    copies[6].wait()
    copies[7].wait()
    for g in range(z.chunks):
        cut = slice(g * size, (g + 1) * size)
        out = dot3(high[cut], low[cut], high_m[...], low_m[...])
        for i in range(z.group):
            block = out[i * z.rows : (i + 1) * z.rows]
            put_halves(keeps[g], sends[g], bit, z.group, i, block, z.half)


def rotated(value, near, far, k):
    shape = value[0].shape
    fr = jnp.broadcast_to(far[0][:, k : k + 1], shape)
    fi = jnp.broadcast_to(far[1][:, k : k + 1], shape)
    nr, ni = near[0], near[1]
    rr, ri = nr * fr - ni * fi, nr * fi + ni * fr
    return value[0] * rr - value[1] * ri, value[0] * ri + value[1] * rr


def blended(z, level, chunk, keep, arrived, near, far, wide_high, wide_low, high, low):
    close = near[level, 0], near[level, 1]
    steps = far[level, 0], far[level, 1]
    for i in range(z.group):
        value = tuple(
            jnp.concatenate([keep[part * z.group + i], arrived[part * z.group + i]], axis=0)
            for part in range(2)
        )
        value = rotated(value, close, steps, chunk * z.group + i)
        put_split(high, low, i * z.rows, z.rows, value)
    return dot3(wide_high[level], wide_low[level], high[...], low[...])


def level_kernel(z, level, chunk, riding, kept, arrived, *refs):
    packs, refs = refs[:riding], refs[riding:]
    near, far, wide_high, wide_low, keep, send, high, low = refs
    bit = lax.axis_index("sub") >> (level + 1) & 1
    out = blended(z, level, chunk, kept, arrived, near, far, wide_high, wide_low, high, low)
    for i in range(z.group):
        put_halves(keep, send, bit, z.group, i, out[i * z.rows : (i + 1) * z.rows], z.half)
    if riding:
        known = packs[0][z.rows :] + packs[1][z.rows :]
        send[2 * z.group :] = known.reshape(-1, z.half, LANES)


def return_kernel(
    z, chunk, kept, arrived, near, far, wide_high, wide_low, last_near, last_far,
    high_m, low_m, twiddle, back, high, low,
):
    out = blended(z, z.last - 1, chunk, kept, arrived, near, far, wide_high, wide_low, high, low)
    close = last_near[0], last_near[1]
    steps = last_far[0], last_far[1]
    for i in range(z.group):
        block = out[i * z.rows : (i + 1) * z.rows]
        value = rotated((block[:, :LANES], block[:, LANES:]), close, steps, chunk * z.group + i)
        put_split(high, low, i * z.rows, z.rows, value)
    out = dot3(high[...], low[...], high_m[...], low_m[...])
    for i in range(z.group):
        k = chunk * z.group + i
        block = out[i * z.rows : (i + 1) * z.rows]
        real, imag = block[:, :LANES], block[:, LANES:]
        c, s = twiddle[0, k : k + 1, :], twiddle[1, k : k + 1, :]
        back[0, i] = real * c - imag * s
        back[1, i] = real * s + imag * c


def gather_back(z, backs, store, mid):
    def load(k):
        back, i = backs[k // z.group], k % z.group
        return back[0, i], back[1, i]

    staged_dft(z.outer, 1, load, store, mid)


def ranges_kernel(z, *refs):
    backs, out_ref, mid = refs[: z.chunks], refs[z.chunks], refs[z.chunks + 1]

    def store(q, value):
        for part in range(2):
            out_ref[q, part] = value[part]

    gather_back(z, backs, store, mid)


def deal_kernel(z, per_block, riding, *refs):
    pairs = z.sub_count // 2
    lines = 2 * per_block * z.rows
    backs, refs = refs[: z.chunks], refs[z.chunks :]
    sent, arrived, refs = refs[0], refs[1], refs[2:]
    outs, (records, mid, whole) = refs[:pairs], refs[pairs:]

    def store(q, value):
        for part in range(2):
            at = (part * per_block + q % per_block) * z.rows
            whole[q // per_block, at : at + z.rows] = value[part]

    gather_back(z, backs, store, mid)
    me = lax.axis_index("sub")
    for k in range(pairs):
        for side in range(2):
            outs[k][side * lines : (side + 1) * lines] = whole[me ^ (2 * k + side)]
    known = (sent[2 * z.group :] + arrived[2 * z.group :]).reshape(-1, LANES)
    records[...] = known
    if riding:
        outs[1][2 * lines :] = known


def stack_kernel(lines, count, *refs):
    for i, ref in enumerate(refs[:count]):
        refs[-1][i * lines : (i + 1) * lines] = ref[lines : 2 * lines]
    if len(refs) > count + 1:
        known = refs[count][...]
        for ref in refs[count + 1 : -1]:
            known = known + ref[2 * lines :]
        refs[-1][count * lines :] = known


def turn_kernel(z, per_block, places, *refs):
    blend_high, blend_low, out_ref = refs[-3:]
    for part in range(2 * per_block):
        line = []
        for array, at in places:
            at += part * z.rows
            line.append(refs[array][at : at + z.rows])
        line = jnp.concatenate(line, axis=0).T
        high = line.astype(bf16)
        low = (line - high.astype(f32)).astype(bf16)
        a, cut = part // per_block, part % per_block
        out_ref[a, cut * LANES : (cut + 1) * LANES, :] = dot3(high, low, blend_high[...], blend_low[...])


def pair_order(pairs):
    return [*range(pairs // 2, pairs), *range(1, pairs // 2)]


def body(sub_images, shift_table, phase_table, offset_table, weight_table):
    _, rows, range_bins = sub_images.shape
    outer = range_bins // LANES
    sub_count = lax.axis_size("sub")
    z = Sizes(rows, outer, weight_table.shape[3], sub_count)
    size = z.group * rows
    flops = 3 * 2 * size * MXU * MXU
    shape = jax.ShapeDtypeStruct
    mid = pltpu.VMEM((2, outer, rows, LANES), f32)
    halves = [pltpu.VMEM((size, 2 * LANES), bf16)] * 2
    slab = shape((2 * z.group, z.half, LANES), f32)

    sources = [shift_table, phase_table, offset_table, weight_table, sub_images]
    sources += [jnp.asarray(table) for table in (lane_twiddle(outer, -1), *lane_matrix(-1, 1.0))]
    sources = [pltpu.with_memory_space_constraint(source, pltpu.HBM) for source in sources]
    tabs, pack, *parts = call(
        functools.partial(start_kernel, z),
        [shape((rows, z.pages * LANES), f32), shape((rows + z.blocks * z.record, LANES), f32)]
        + [slab] * (2 * z.chunks),
        sources,
        [pltpu.VMEM(source.shape, source.dtype) for source in sources]
        + [pltpu.VMEM((z.pages * LANES, LANES), f32), mid]
        + [pltpu.VMEM((outer * rows, 2 * LANES), bf16)] * 2
        + [pltpu.SemaphoreType.DMA((len(sources),))],
        flops * z.chunks,
        space=pltpu.HBM,
    )
    keeps, sends = parts[: z.chunks], parts[z.chunks :]
    arrived = [swapped(send, "sub", 0) for send in sends]
    tables = call(
        functools.partial(tables_kernel, z),
        [shape((z.last, 2, rows, LANES), f32)] * 2 + [shape((z.last, size, size), bf16)] * 2,
        [tabs],
        [],
        1 << 20,
    )
    other = swapped(pack, "sub", z.last)
    tail = z.blocks * z.record
    longer = shape((2 * z.group + tail // z.half, z.half, LANES), f32)
    for level in range(z.last - 1):
        for chunk in range(z.chunks):
            rides = level == z.last - 2 and chunk == z.chunks - 1
            keeps[chunk], sends[chunk] = call(
                functools.partial(level_kernel, z, level, chunk, 2 * rides),
                [slab, longer if rides else slab],
                [keeps[chunk], arrived[chunk]] + [pack, other] * rides + list(tables),
                halves,
                flops,
            )
            arrived[chunk] = swapped(sends[chunk], "sub", level + 1)
    last_tables = call(
        functools.partial(last_tables_kernel, z),
        [shape((2, rows, LANES), f32)] * 2,
        [pack, other],
        [],
        1 << 16,
    )
    way_back = [*lane_matrix(1, 1.0 / range_bins), lane_twiddle(outer, 1)]
    backs = [
        call(
            functools.partial(return_kernel, z, chunk),
            [shape((2, z.group, rows, LANES), f32)],
            [keeps[chunk], arrived[chunk], *tables, *last_tables, *way_back],
            halves,
            2 * flops,
        )[0]
        for chunk in range(z.chunks)
    ]
    block = range_bins // sub_count
    beams = sub_count * rows
    if block % LANES or beams > MXU or sub_count < 8:
        (children,) = call(
            functools.partial(ranges_kernel, z),
            [shape((outer, 2, rows, LANES), f32)],
            backs,
            [mid],
            flops,
        )
        known = (sends[-1] + arrived[-1])[2 * z.group :].reshape(-1, LANES)
        for level in range(z.last - 1):
            known = known + swapped(known, "sub", level)
        return wide_turn(z, block, children, known)

    per_block = block // LANES
    pairs = sub_count // 2
    lines = 2 * per_block * rows
    riding = z.last > 2
    *messages, known = call(
        functools.partial(deal_kernel, z, per_block, riding),
        [shape((2 * lines + (tail if riding and k == 1 else 0), LANES), f32) for k in range(pairs)]
        + [shape((tail, LANES), f32)],
        [*backs, sends[-1], arrived[-1]],
        [mid, pltpu.VMEM((sub_count, lines, LANES), f32)],
        flops,
    )
    arrays = [messages[0]] + [None] * (pairs - 1)
    for k in pair_order(pairs):
        route = [(i, i ^ (2 * k)) for i in range(sub_count)]
        arrays[k] = lax.ppermute(messages[k], "sub", route)
    places = {2 * k: (k, 0) for k in range(pairs)}
    cuts = [list(range(pairs // 2)), list(range(pairs // 2, pairs))]
    crossing = []
    for cut in cuts:
        records = [] if crossing else [known] + [arrays[1]] * riding
        (both,) = call(
            functools.partial(stack_kernel, lines, len(cut)),
            [shape((len(cut) * lines + tail * bool(records), LANES), f32)],
            [arrays[k] for k in cut] + records,
            [],
            1,
        )
        places.update({2 * k + 1: (len(arrays), i * lines) for i, k in enumerate(cut)})
        crossing.append(both)
        arrays.append(swapped(both, "sub", 0))
    blend = call(
        functools.partial(last_blend_kernel, z),
        [shape((beams, beams), bf16)] * 2,
        [crossing[0], arrays[pairs]],
        [],
        1 << 18,
    )
    (turned,) = call(
        functools.partial(turn_kernel, z, per_block, [places[away] for away in range(sub_count)]),
        [shape((2, block, beams), f32)],
        [*arrays, *blend],
        [],
        flops,
    )
    return turned


def wide_turn(z, block, children, known):
    sub_count, rows, half = z.sub_count, z.rows, z.half
    if block % LANES == 0:
        line = children.reshape(sub_count, block // LANES, 2, rows, LANES).transpose(0, 2, 3, 1, 4)
    else:
        line = children.reshape(z.outer, 2, rows, LANES // block, block).transpose(0, 3, 1, 2, 4)
    gathered = lax.all_to_all(line.reshape(sub_count, 2 * rows, block), "sub", 0, 0, tiled=True)
    gathered = gathered.reshape(sub_count, 2, 2, half, block)
    table = known.reshape(z.blocks, z.record, z.slots, rows).transpose(0, 2, 1, 3)
    table = table.reshape(-1, z.record, rows)[:sub_count]
    weights = table[:, : z.at_offset].reshape(sub_count, 2, z.taps, rows)
    offsets = table[:, z.at_offset : z.at_shift].astype(jnp.int32)
    columns = jnp.arange(half, dtype=jnp.int32)
    stencil = 0.0
    for tap in range(z.taps):
        hits = columns == offsets[..., None] + tap
        stencil = stencil + jnp.where(hits, weights[:, :, tap, :, None], 0.0)
    index = jnp.arange(sub_count, dtype=jnp.int32)
    side = (index >> z.last & 1)[:, None, None, None]
    chosen = jnp.where(side == 0, gathered[:, :, 0], gathered[:, :, 1])
    crossing = gathered[index ^ (1 << z.last)]
    crossing = jnp.where(side == 0, crossing[:, :, 0], crossing[:, :, 1])
    both = jnp.concatenate([chosen, crossing], axis=2)
    matrix = jnp.moveaxis(stencil, 1, 2).reshape(sub_count, rows, rows)
    merged = jnp.einsum("ijm,ipmq->pqij", matrix, both, precision=lax.Precision.HIGHEST)
    return merged.reshape(2, block, sub_count * rows)


def solution(mesh):
    placed = (
        P(None, ("img", "sub"), None),
        P(None, "sub", None, None),
        P(None, "sub", None, None),
        P(None, "sub", None, None),
        P(None, "sub", None, None, None),
    )

    return jax.shard_map(
        body, mesh=mesh, in_specs=placed, out_specs=P(None, ("img", "sub"), None), check_vma=False
    )
```

profile of v0, /device:TPU:0, one launch (start us, length us, event | category | flops | bytes accessed | tf_op | source)
XLA Modules:
  0.0 42.1 jit_solution(1917752517957316153)
XLA Ops:
  0.0 1.8 %shard_map.109 = (f32[16,128]{1,0:T(8,128)S(1)}, f32[48,128]{1,0:T(8,128)S(1)}, f32[32,8,128]{2,1,0:T(8,128)S(1)}, f32[32,8,128]{2,1,0:T(8,128)S(1)}, f32[32,8,1...) custom-call(s32[4,1,2,8]{3,2,1,0:T(2,128)} %refs_0_.1, f32[4,1,2,8]{3,2,1,0:T(2,128)} %refs_1_.1, s32[4,1,2,16]{3,2,1,0:T(2,128)} %refs_2_.1, ...), custom_call_target="tpu_custom_call" | custom-call | flops 201326592 | bytes 1379328 | tf_op jit(solution)/shard_map/pallas_call | solution.py:39
  1.8 0.6 %collective-permute-start = (f32[32,8,128]{2,1,0:T(8,128)S(1)}, f32[32,8,128]{2,1,0:T(8,128)S(1)}, u32[]{:S(2)}, u32[]{:S(2)}) collective-permute-start(f32[32,8,128]{2,1,0:T(8,128)S(1)} %get-tuple-element.37), channel_id=1, source_target_pairs={{0,1},{1,0},{2,3},{3,2},{4,5},{5,4},{6,7},{7,6},{8,9},{9,8},{10,11... | collective-permute-start | bytes 393224 | tf_op jit(solution)/shard_map/ppermute | solution.py:28
  2.4 0.1 collective-permute-start.4
  2.5 0.4 shard_map.110
  2.9 0.5 %collective-permute-done.refs_1_ = f32[32,8,128]{2,1,0:T(8,128)S(1)} collective-permute-done((f32[32,8,128]{2,1,0:T(8,128)S(1)}, f32[32,8,128]{2,1,0:T(8,128)S(1)}, u32[]{:S(2)}, u32[]{:S(2)}) %collective-permute-start) | collective-permute-done | bytes 131104 | tf_op jit(solution)/shard_map/ppermute | solution.py:28
  3.4 0.4 %shard_map.111 = (f32[32,8,128]{2,1,0:T(8,128)S(1)}, f32[32,8,128]{2,1,0:T(8,128)S(1)}) custom-call(f32[32,8,128]{2,1,0:T(8,128)S(1)} %get-tuple-element.36.refs_0_, f32[32,8,128]{2,1,0:T(8,128)S(1)} %collective-permute-done.refs_1_, f32[3,2,16,128]{3,2,1,0:T(8,128)S(1)} %get-tuple-element.39.refs_2_.refs_4_, ...), custom_call_target="tpu_custom_call" | custom-call | flops 100663296 | bytes 1409024 | tf_op jit(solution)/shard_map/pallas_call | solution.py:39
  3.8 2.9 %collective-permute-start.1 = (f32[32,8,128]{2,1,0:T(8,128)S(1)}, f32[32,8,128]{2,1,0:T(8,128)S(1)}, u32[]{:S(2)}, u32[]{:S(2)}) collective-permute-start(f32[32,8,128]{2,1,0:T(8,128)S(1)} %get-tuple-element.44), channel_id=1, source_target_pairs={{0,2},{2,0},{1,3},{3,1},{4,6},{6,4},{5,7},{7,5},{8,10},{10,8},{9,1... | collective-permute-start | bytes 393224 | tf_op jit(solution)/shard_map/ppermute | solution.py:28
  6.8 0.0 collective-permute-done.4.refs_1_
  6.8 0.4 %shard_map.115 = (f32[32,8,128]{2,1,0:T(8,128)S(1)}, f32[32,8,128]{2,1,0:T(8,128)S(1)}) custom-call(f32[32,8,128]{2,1,0:T(8,128)S(1)} %get-tuple-element.50.refs_0_, f32[32,8,128]{2,1,0:T(8,128)S(1)} %collective-permute-done.4.refs_1_, f32[3,2,16,128]{3,2,1,0:T(8,128)S(1)} %get-tuple-element.39.refs_2_.refs_4_, ...), custom_call_target="tpu_custom_call" | custom-call | flops 100663296 | bytes 1409024 | tf_op jit(solution)/shard_map/pallas_call | solution.py:39
  7.2 0.1 collective-permute-start.5
  7.3 3.1 %collective-permute-start.3 = (f32[48,128]{1,0:T(8,128)S(1)}, f32[48,128]{1,0:T(8,128)S(1)}, u32[]{:S(2)}, u32[]{:S(2)}) collective-permute-start(f32[48,128]{1,0:T(8,128)S(1)} %get-tuple-element.47.refs_0_.refs_2_), channel_id=1, source_target_pairs={{0,8},{8,0},{1,9},{9,1},{2,10},{10,2},{3,11},{11,3},{4,12},{12,4},... | collective-permute-start | bytes 73736 | tf_op jit(solution)/shard_map/ppermute | solution.py:28
  10.4 0.7 %collective-permute-done.1.refs_1_ = f32[32,8,128]{2,1,0:T(8,128)S(1)} collective-permute-done((f32[32,8,128]{2,1,0:T(8,128)S(1)}, f32[32,8,128]{2,1,0:T(8,128)S(1)}, u32[]{:S(2)}, u32[]{:S(2)}) %collective-permute-start.1) | collective-permute-done | bytes 131104 | tf_op jit(solution)/shard_map/ppermute | solution.py:28
  11.1 0.4 %shard_map.112 = (f32[32,8,128]{2,1,0:T(8,128)S(1)}, f32[32,8,128]{2,1,0:T(8,128)S(1)}) custom-call(f32[32,8,128]{2,1,0:T(8,128)S(1)} %get-tuple-element.43.refs_0_, f32[32,8,128]{2,1,0:T(8,128)S(1)} %collective-permute-done.1.refs_1_, f32[3,2,16,128]{3,2,1,0:T(8,128)S(1)} %get-tuple-element.39.refs_2_.refs_4_, ...), custom_call_target="tpu_custom_call" | custom-call | flops 100663296 | bytes 1409024 | tf_op jit(solution)/shard_map/pallas_call | solution.py:39
  11.6 2.1 %collective-permute-start.2 = (f32[32,8,128]{2,1,0:T(8,128)S(1)}, f32[32,8,128]{2,1,0:T(8,128)S(1)}, u32[]{:S(2)}, u32[]{:S(2)}) collective-permute-start(f32[32,8,128]{2,1,0:T(8,128)S(1)} %get-tuple-element.46), channel_id=1, source_target_pairs={{0,4},{4,0},{1,5},{5,1},{2,6},{6,2},{3,7},{7,3},{8,12},{12,8},{9,1... | collective-permute-start | bytes 393224 | tf_op jit(solution)/shard_map/ppermute | solution.py:28
  13.7 0.0 collective-permute-done.3.refs_1_.refs_3_
  13.7 0.0 collective-permute-done.5.refs_1_
  13.7 0.0 copy-start
  13.7 0.0 copy-start.1
  13.7 0.4 %shard_map.116 = (f32[32,8,128]{2,1,0:T(8,128)S(1)}, f32[36,8,128]{2,1,0:T(8,128)S(1)}) custom-call(f32[32,8,128]{2,1,0:T(8,128)S(1)} %get-tuple-element.52.refs_0_, f32[32,8,128]{2,1,0:T(8,128)S(1)} %collective-permute-done.5.refs_1_, f32[48,128]{1,0:T(8,128)S(1)} %get-tuple-element.47.refs_0_.refs_2_, ...), custom_call_target="tpu_custom_call" | custom-call | flops 100663296 | bytes 1474560 | tf_op jit(solution)/shard_map/pallas_call | solution.py:39
  14.2 0.0 copy-start.2
  14.2 1.5 %collective-permute-start.6 = (f32[36,8,128]{2,1,0:T(8,128)S(1)}, f32[36,8,128]{2,1,0:T(8,128)S(1)}, u32[]{:S(2)}, u32[]{:S(2)}) collective-permute-start(f32[36,8,128]{2,1,0:T(8,128)S(1)} %get-tuple-element.55.refs_2_), channel_id=1, source_target_pairs={{0,4},{4,0},{1,5},{5,1},{2,6},{6,2},{3,7},{7,3},{8,12},{12,8},{9,1... | collective-permute-start | bytes 442376 | tf_op jit(solution)/shard_map/ppermute | solution.py:28
  15.7 0.2 shard_map.113
  16.0 1.3 %collective-permute-done.2.refs_1_ = f32[32,8,128]{2,1,0:T(8,128)S(1)} collective-permute-done((f32[32,8,128]{2,1,0:T(8,128)S(1)}, f32[32,8,128]{2,1,0:T(8,128)S(1)}, u32[]{:S(2)}, u32[]{:S(2)}) %collective-permute-start.2) | collective-permute-done | bytes 131104 | tf_op jit(solution)/shard_map/ppermute | solution.py:28
  17.3 0.0 copy-done
  17.3 0.0 copy-done.1
  17.3 0.0 copy-done.2
  17.3 0.8 %shard_map.114.refs_0_ = f32[2,16,16,128]{3,2,1,0:T(8,128)S(1)} custom-call(f32[32,8,128]{2,1,0:T(8,128)S(1)} %get-tuple-element.45.refs_0_, f32[32,8,128]{2,1,0:T(8,128)S(1)} %collective-permute-done.2.refs_1_, f32[3,2,16,128]{3,2,1,0:T(8,128)S(1)} %get-tuple-element.39.refs_2_.refs_4_, f32[3,2,16,128]{3,2,1,0:T(8,128)S(1)} %get-tuple-element.40.refs_3_.refs_5_, ...), custom_call_target="tpu_custom_call" | custom-call | flops 201326592 | bytes 1736704 | tf_op jit(solution)/shard_map/pallas_call | solution.py:39
  18.1 1.7 %collective-permute-done.6.refs_1_.refs_3_ = f32[36,8,128]{2,1,0:T(8,128)S(1)} collective-permute-done((f32[36,8,128]{2,1,0:T(8,128)S(1)}, f32[36,8,128]{2,1,0:T(8,128)S(1)}, u32[]{:S(2)}, u32[]{:S(2)}) %collective-permute-start.6) | collective-permute-done | bytes 147488 | tf_op jit(solution)/shard_map/ppermute | solution.py:28
  19.8 0.8 %shard_map.117.refs_1_ = f32[2,16,16,128]{3,2,1,0:T(8,128)S(1)} custom-call(f32[32,8,128]{2,1,0:T(8,128)S(1)} %get-tuple-element.54.refs_0_, f32[36,8,128]{2,1,0:T(8,128)S(1)} %collective-permute-done.6.refs_1_.refs_3_, f32[3,2,16,128]{3,2,1,0:T(8,128)S(1)} %get-tuple-element.39.refs_2_.refs_4_, f32[3,2,16,128]{3,2,1,0:T(8,128)S(1)} %get-tuple-element.40.refs_3_.refs_5_, ...), custom_call_target="tpu_custom_call" | custom-call | flops 201326592 | bytes 1753088 | tf_op jit(solution)/shard_map/pallas_call | solution.py:39
  20.6 0.2 shard_map.118
  20.8 2.1 %collective-permute-start.8 = (f32[128,128]{1,0:T(8,128)S(1)}, f32[128,128]{1,0:T(8,128)S(1)}, u32[]{:S(2)}, u32[]{:S(2)}) collective-permute-start(f32[128,128]{1,0:T(8,128)S(1)} %get-tuple-element.58), channel_id=1, source_target_pairs={{0,4},{1,5},{2,6},{3,7},{4,0},{5,1},{6,2},{7,3},{8,12},{9,13},{10,... | collective-permute-start | bytes 196616 | tf_op jit(solution)/shard_map/ppermute | solution.py:562
  22.9 1.4 %collective-permute-start.9 = (f32[128,128]{1,0:T(8,128)S(1)}, f32[128,128]{1,0:T(8,128)S(1)}, u32[]{:S(2)}, u32[]{:S(2)}) collective-permute-start(f32[128,128]{1,0:T(8,128)S(1)} %get-tuple-element.59), channel_id=1, source_target_pairs={{0,6},{1,7},{2,4},{3,5},{4,2},{5,3},{6,0},{7,1},{8,14},{9,15},{10,... | collective-permute-start | bytes 196616 | tf_op jit(solution)/shard_map/ppermute | solution.py:562
  24.3 0.1 collective-permute-start.7
  24.5 3.0 %collective-permute-start.10 = (f32[128,128]{1,0:T(8,128)S(1)}, f32[128,128]{1,0:T(8,128)S(1)}, u32[]{:S(2)}, u32[]{:S(2)}) collective-permute-start(f32[128,128]{1,0:T(8,128)S(1)} %get-tuple-element.60), channel_id=1, source_target_pairs={{0,8},{1,9},{2,10},{3,11},{4,12},{5,13},{6,14},{7,15},{8,0},{9,1},... | collective-permute-start | bytes 196616 | tf_op jit(solution)/shard_map/ppermute | solution.py:562
  27.4 1.3 %collective-permute-start.11 = (f32[128,128]{1,0:T(8,128)S(1)}, f32[128,128]{1,0:T(8,128)S(1)}, u32[]{:S(2)}, u32[]{:S(2)}) collective-permute-start(f32[128,128]{1,0:T(8,128)S(1)} %get-tuple-element.61), channel_id=1, source_target_pairs={{0,10},{1,11},{2,8},{3,9},{4,14},{5,15},{6,12},{7,13},{8,2},{9,3},... | collective-permute-start | bytes 196616 | tf_op jit(solution)/shard_map/ppermute | solution.py:562
  28.7 0.0 collective-permute-done.8.refs_2_
  28.7 3.6 %collective-permute-start.12 = (f32[128,128]{1,0:T(8,128)S(1)}, f32[128,128]{1,0:T(8,128)S(1)}, u32[]{:S(2)}, u32[]{:S(2)}) collective-permute-start(f32[128,128]{1,0:T(8,128)S(1)} %get-tuple-element.62), channel_id=1, source_target_pairs={{0,12},{1,13},{2,14},{3,15},{4,8},{5,9},{6,10},{7,11},{8,4},{9,5},... | collective-permute-start | bytes 196616 | tf_op jit(solution)/shard_map/ppermute | solution.py:562
  32.3 0.0 collective-permute-done.9.refs_3_
  32.3 0.0 collective-permute-start.13
  32.3 0.0 collective-permute-done.7.refs_1_.refs_5_
  32.3 0.1 collective-permute-start.14
  32.4 0.0 collective-permute-done.10.refs_0_.refs_4_
  32.4 4.8 %collective-permute-done.11.refs_1_.refs_5_ = f32[128,128]{1,0:T(8,128)S(1)} collective-permute-done((f32[128,128]{1,0:T(8,128)S(1)}, f32[128,128]{1,0:T(8,128)S(1)}, u32[]{:S(2)}, u32[]{:S(2)}) %collective-permute-start.11) | collective-permute-done | bytes 65568 | tf_op jit(solution)/shard_map/ppermute | solution.py:562
  37.3 0.0 collective-permute-done.12.refs_2_.refs_6_
  37.3 2.1 %collective-permute-done.13.refs_3_.refs_7_ = f32[128,128]{1,0:T(8,128)S(1)} collective-permute-done((f32[128,128]{1,0:T(8,128)S(1)}, f32[128,128]{1,0:T(8,128)S(1)}, u32[]{:S(2)}, u32[]{:S(2)}) %collective-permute-start.13) | collective-permute-done | bytes 65568 | tf_op jit(solution)/shard_map/ppermute | solution.py:562
  39.4 0.1 collective-permute-start.15
  39.5 0.0 collective-permute-done.14.refs_1_.refs_8_
  39.5 0.1 shard_map.121
  39.6 1.2 %collective-permute-done.15.refs_9_ = f32[256,128]{1,0:T(8,128)S(1)} collective-permute-done((f32[256,128]{1,0:T(8,128)S(1)}, f32[256,128]{1,0:T(8,128)S(1)}, u32[]{:S(2)}, u32[]{:S(2)}) %collective-permute-start.15) | collective-permute-done | bytes 131104 | tf_op jit(solution)/shard_map/ppermute | solution.py:28
  40.8 1.2 %shard_map.122 = f32[2,256,256]{2,1,0:T(8,128)} custom-call(f32[128,128]{1,0:T(8,128)S(1)} %get-tuple-element.56.refs_0_, f32[160,128]{1,0:T(8,128)S(1)} %collective-permute-done.7.refs_1_.refs_5_, f32[128,128]{1,0:T(8,128)S(1)} %collective-permute-done.8.refs_2_, f32[128,128]{1,0:T(8,128)S(1)} %collective-permute-done.9.refs_3_, ...), custom_call_target="tpu_custom_call" | custom-call | flops 100663296 | bytes 1605632 | tf_op jit(solution)/shard_map/pallas_call | solution.py:39
  (2 shorter events, 0.0 us)
Async XLA Ops:
  1.8 1.5 %collective-permute-start = (f32[32,8,128]{2,1,0:T(8,128)S(1)}, f32[32,8,128]{2,1,0:T(8,128)S(1)}, u32[]{:S(2)}, u32[]{:S(2)}) collective-permute-start(f32[32,8,128]{2,1,0:T(8,128)S(1)} %get-tuple-element.37), channel_id=1, source_target_pairs={{0,1},{1,0},{2,3},{3,2},{4,5},{5,4},{6,7},{7,6},{8,9},{9,8},{10,11... | collective-permute-start | bytes 393224 | tf_op jit(solution)/shard_map/ppermute | solution.py:28
  2.4 4.4 %collective-permute-start.4 = (f32[32,8,128]{2,1,0:T(8,128)S(1)}, f32[32,8,128]{2,1,0:T(8,128)S(1)}, u32[]{:S(2)}, u32[]{:S(2)}) collective-permute-start(f32[32,8,128]{2,1,0:T(8,128)S(1)} %get-tuple-element.51), channel_id=1, source_target_pairs={{0,1},{1,0},{2,3},{3,2},{4,5},{5,4},{6,7},{7,6},{8,9},{9,8},{10,11... | collective-permute-start | bytes 393224 | tf_op jit(solution)/shard_map/ppermute | solution.py:28
  3.8 7.3 %collective-permute-start.1 = (f32[32,8,128]{2,1,0:T(8,128)S(1)}, f32[32,8,128]{2,1,0:T(8,128)S(1)}, u32[]{:S(2)}, u32[]{:S(2)}) collective-permute-start(f32[32,8,128]{2,1,0:T(8,128)S(1)} %get-tuple-element.44), channel_id=1, source_target_pairs={{0,2},{2,0},{1,3},{3,1},{4,6},{6,4},{5,7},{7,5},{8,10},{10,8},{9,1... | collective-permute-start | bytes 393224 | tf_op jit(solution)/shard_map/ppermute | solution.py:28
  7.2 6.5 %collective-permute-start.5 = (f32[32,8,128]{2,1,0:T(8,128)S(1)}, f32[32,8,128]{2,1,0:T(8,128)S(1)}, u32[]{:S(2)}, u32[]{:S(2)}) collective-permute-start(f32[32,8,128]{2,1,0:T(8,128)S(1)} %get-tuple-element.53), channel_id=1, source_target_pairs={{0,2},{2,0},{1,3},{3,1},{4,6},{6,4},{5,7},{7,5},{8,10},{10,8},{9,1... | collective-permute-start | bytes 393224 | tf_op jit(solution)/shard_map/ppermute | solution.py:28
  7.3 6.4 %collective-permute-start.3 = (f32[48,128]{1,0:T(8,128)S(1)}, f32[48,128]{1,0:T(8,128)S(1)}, u32[]{:S(2)}, u32[]{:S(2)}) collective-permute-start(f32[48,128]{1,0:T(8,128)S(1)} %get-tuple-element.47.refs_0_.refs_2_), channel_id=1, source_target_pairs={{0,8},{8,0},{1,9},{9,1},{2,10},{10,2},{3,11},{11,3},{4,12},{12,4},... | collective-permute-start | bytes 73736 | tf_op jit(solution)/shard_map/ppermute | solution.py:28
  11.6 5.7 %collective-permute-start.2 = (f32[32,8,128]{2,1,0:T(8,128)S(1)}, f32[32,8,128]{2,1,0:T(8,128)S(1)}, u32[]{:S(2)}, u32[]{:S(2)}) collective-permute-start(f32[32,8,128]{2,1,0:T(8,128)S(1)} %get-tuple-element.46), channel_id=1, source_target_pairs={{0,4},{4,0},{1,5},{5,1},{2,6},{6,2},{3,7},{7,3},{8,12},{12,8},{9,1... | collective-permute-start | bytes 393224 | tf_op jit(solution)/shard_map/ppermute | solution.py:28
  13.7 3.6 %copy-start = (bf16[256,256]{1,0:T(8,128)(2,1)S(1)}, bf16[256,256]{1,0:T(8,128)(2,1)}, u32[]{:S(2)}) copy-start(bf16[256,256]{1,0:T(8,128)(2,1)} %constant.16.clone.refs_9_) | copy-start | bytes 393220
  13.7 3.5 %copy-start.1 = (bf16[256,256]{1,0:T(8,128)(2,1)S(1)}, bf16[256,256]{1,0:T(8,128)(2,1)}, u32[]{:S(2)}) copy-start(bf16[256,256]{1,0:T(8,128)(2,1)} %constant.15.clone.refs_8_) | copy-start | bytes 393220
  14.2 3.1 %copy-start.2 = (f32[2,32,128]{2,1,0:T(8,128)S(1)}, f32[2,32,128]{2,1,0:T(8,128)}, u32[]{:S(2)}) copy-start(f32[2,32,128]{2,1,0:T(8,128)} %constant.17.clone.refs_10_) | copy-start | bytes 98308
  14.2 5.6 %collective-permute-start.6 = (f32[36,8,128]{2,1,0:T(8,128)S(1)}, f32[36,8,128]{2,1,0:T(8,128)S(1)}, u32[]{:S(2)}, u32[]{:S(2)}) collective-permute-start(f32[36,8,128]{2,1,0:T(8,128)S(1)} %get-tuple-element.55.refs_2_), channel_id=1, source_target_pairs={{0,4},{4,0},{1,5},{5,1},{2,6},{6,2},{3,7},{7,3},{8,12},{12,8},{9,1... | collective-permute-start | bytes 442376 | tf_op jit(solution)/shard_map/ppermute | solution.py:28
  20.8 7.9 %collective-permute-start.8 = (f32[128,128]{1,0:T(8,128)S(1)}, f32[128,128]{1,0:T(8,128)S(1)}, u32[]{:S(2)}, u32[]{:S(2)}) collective-permute-start(f32[128,128]{1,0:T(8,128)S(1)} %get-tuple-element.58), channel_id=1, source_target_pairs={{0,4},{1,5},{2,6},{3,7},{4,0},{5,1},{6,2},{7,3},{8,12},{9,13},{10,... | collective-permute-start | bytes 196616 | tf_op jit(solution)/shard_map/ppermute | solution.py:562
  22.9 9.4 %collective-permute-start.9 = (f32[128,128]{1,0:T(8,128)S(1)}, f32[128,128]{1,0:T(8,128)S(1)}, u32[]{:S(2)}, u32[]{:S(2)}) collective-permute-start(f32[128,128]{1,0:T(8,128)S(1)} %get-tuple-element.59), channel_id=1, source_target_pairs={{0,6},{1,7},{2,4},{3,5},{4,2},{5,3},{6,0},{7,1},{8,14},{9,15},{10,... | collective-permute-start | bytes 196616 | tf_op jit(solution)/shard_map/ppermute | solution.py:562
  24.3 8.0 %collective-permute-start.7 = (f32[160,128]{1,0:T(8,128)S(1)}, f32[160,128]{1,0:T(8,128)S(1)}, u32[]{:S(2)}, u32[]{:S(2)}) collective-permute-start(f32[160,128]{1,0:T(8,128)S(1)} %get-tuple-element.57), channel_id=1, source_target_pairs={{0,2},{1,3},{2,0},{3,1},{4,6},{5,7},{6,4},{7,5},{8,10},{9,11},{10,... | collective-permute-start | bytes 245768 | tf_op jit(solution)/shard_map/ppermute | solution.py:562
  24.5 8.0 %collective-permute-start.10 = (f32[128,128]{1,0:T(8,128)S(1)}, f32[128,128]{1,0:T(8,128)S(1)}, u32[]{:S(2)}, u32[]{:S(2)}) collective-permute-start(f32[128,128]{1,0:T(8,128)S(1)} %get-tuple-element.60), channel_id=1, source_target_pairs={{0,8},{1,9},{2,10},{3,11},{4,12},{5,13},{6,14},{7,15},{8,0},{9,1},... | collective-permute-start | bytes 196616 | tf_op jit(solution)/shard_map/ppermute | solution.py:562
  27.4 9.8 %collective-permute-start.11 = (f32[128,128]{1,0:T(8,128)S(1)}, f32[128,128]{1,0:T(8,128)S(1)}, u32[]{:S(2)}, u32[]{:S(2)}) collective-permute-start(f32[128,128]{1,0:T(8,128)S(1)} %get-tuple-element.61), channel_id=1, source_target_pairs={{0,10},{1,11},{2,8},{3,9},{4,14},{5,15},{6,12},{7,13},{8,2},{9,3},... | collective-permute-start | bytes 196616 | tf_op jit(solution)/shard_map/ppermute | solution.py:562
  28.7 8.6 %collective-permute-start.12 = (f32[128,128]{1,0:T(8,128)S(1)}, f32[128,128]{1,0:T(8,128)S(1)}, u32[]{:S(2)}, u32[]{:S(2)}) collective-permute-start(f32[128,128]{1,0:T(8,128)S(1)} %get-tuple-element.62), channel_id=1, source_target_pairs={{0,12},{1,13},{2,14},{3,15},{4,8},{5,9},{6,10},{7,11},{8,4},{9,5},... | collective-permute-start | bytes 196616 | tf_op jit(solution)/shard_map/ppermute | solution.py:562
  32.3 7.1 %collective-permute-start.13 = (f32[128,128]{1,0:T(8,128)S(1)}, f32[128,128]{1,0:T(8,128)S(1)}, u32[]{:S(2)}, u32[]{:S(2)}) collective-permute-start(f32[128,128]{1,0:T(8,128)S(1)} %get-tuple-element.63), channel_id=1, source_target_pairs={{0,14},{1,15},{2,12},{3,13},{4,10},{5,11},{6,8},{7,9},{8,6},{9,7},... | collective-permute-start | bytes 196616 | tf_op jit(solution)/shard_map/ppermute | solution.py:562
  32.3 7.1 %collective-permute-start.14 = (f32[288,128]{1,0:T(8,128)S(1)}, f32[288,128]{1,0:T(8,128)S(1)}, u32[]{:S(2)}, u32[]{:S(2)}) collective-permute-start(f32[288,128]{1,0:T(8,128)S(1)} %shard_map.119.refs_0_), channel_id=1, source_target_pairs={{0,1},{1,0},{2,3},{3,2},{4,5},{5,4},{6,7},{7,6},{8,9},{9,8},{10,11... | collective-permute-start | bytes 442376 | tf_op jit(solution)/shard_map/ppermute | solution.py:28
  39.4 1.4 %collective-permute-start.15 = (f32[256,128]{1,0:T(8,128)S(1)}, f32[256,128]{1,0:T(8,128)S(1)}, u32[]{:S(2)}, u32[]{:S(2)}) collective-permute-start(f32[256,128]{1,0:T(8,128)S(1)} %shard_map.120), channel_id=1, source_target_pairs={{0,1},{1,0},{2,3},{3,2},{4,5},{5,4},{6,7},{7,6},{8,9},{9,8},{10,11... | collective-permute-start | bytes 393224 | tf_op jit(solution)/shard_map/ppermute | solution.py:28
where the time goes:
time: 42.2 us; the launch traced here: 42.1 us
  starting transfers between devices  22 us (52%)
  waiting for transfers between devices  12.5 us (30%)
  Pallas kernels  7.41 us (18%)
    ppermute x7, starting transfers between devices, body(): arrays[k] = lax.ppermute(messages[k], 'sub', route)  11.5 us
    ppermute x9, starting transfers between devices, swapped(): return lax.ppermute(block, axis, route)  10.5 us
    pallas_call x14, Pallas kernels, call(): pl.pallas_call(run, out_shape=outs, in_specs=[pl.BlockSpec(memory_space=s...  7.41 us
    ppermute x7, waiting for transfers between devices, body(): arrays[k] = lax.ppermute(messages[k], 'sub', route)  6.95 us
    ppermute x9, waiting for transfers between devices, swapped(): return lax.ppermute(block, axis, route)  5.5 us
  transfers between devices with their start and end apart: 16, of which 7 were waited for; matrix products, arithmetic and copies ran while one was open for 0% of the time, Pallas kernels for 8%

commit v1 on v0

--- a/solution.py
+++ b/solution.py
@@ -28,24 +28,18 @@
     return lax.ppermute(block, axis, route)
 
 
-def call(kernel, outs, ins, scratch, flops, after=(), space=pltpu.VMEM):
+def call(kernel, outs, ins, scratch, flops, space=pltpu.VMEM, out_space=pltpu.VMEM):
     moved = sum(math.prod(o.shape) * o.dtype.itemsize for o in outs)
     moved += sum(math.prod(i.shape) * i.dtype.itemsize for i in ins)
-    count = len(ins)
-
-    def run(*refs):
-        kernel(*refs[:count], *refs[count + len(after) :])
-
     return pl.pallas_call(
-        run,
+        kernel,
         out_shape=outs,
-        in_specs=[pl.BlockSpec(memory_space=space)] * count
-        + [pl.BlockSpec(memory_space=pl.ANY)] * len(after),
-        out_specs=[pl.BlockSpec(memory_space=pltpu.VMEM)] * len(outs),
+        in_specs=[pl.BlockSpec(memory_space=space)] * len(ins),
+        out_specs=[pl.BlockSpec(memory_space=out_space)] * len(outs),
         scratch_shapes=scratch,
         cost_estimate=pl.CostEstimate(flops=flops, bytes_accessed=moved, transcendentals=0),
         compiler_params=pltpu.CompilerParams(vmem_limit_bytes=VMEM_GRANT),
-    )(*ins, *after)
+    )(*ins)
 
 
 def lane_matrix(direction, scale):
@@ -267,7 +261,7 @@
             wide_low[level, i * z.rows : (i + 1) * z.rows] = (value - high.astype(f32)).astype(bf16)
 
 
-def last_blend_kernel(z, ours, theirs, blend_high, blend_low):
+def last_blend_kernel(z, order, ours, theirs, blend_high, blend_low):
     tail = z.blocks * z.record
     known = ours[ours.shape[0] - tail :] + theirs[theirs.shape[0] - tail :]
     me = lax.axis_index("sub")
@@ -287,21 +281,40 @@
                 line = jnp.broadcast_to(table[c * z.taps + tap : c * z.taps + tap + 1], shape)
                 total += jnp.where(hits, line, 0.0)
             parts.append(total)
-        for away in range(z.sub_count):
+        for i, away in enumerate(order):
             source = me ^ away
             value = jnp.where(owner == source, parts[0], 0.0)
             value = jnp.where(owner == (source ^ (1 << z.last)), parts[1], value)
             high = value.astype(bf16)
-            at = (slice(away * z.rows, (away + 1) * z.rows), slice(block * LANES, (block + 1) * LANES))
+            at = (slice(i * z.rows, (i + 1) * z.rows), slice(block * LANES, (block + 1) * LANES))
             blend_high[at] = high
             blend_low[at] = (value - high.astype(f32)).astype(bf16)
 
 
+def forward(z, load, keep, mid, high, low, high_m, low_m, twiddle):
+    held = []
+
+    def store(k, value):
+        c, s = twiddle[0, k : k + 1, :], twiddle[1, k : k + 1, :]
+        held.append((k, (value[0] * c - value[1] * s, value[0] * s + value[1] * c)))
+        if len(held) % 2 == 0:
+            pair = tuple(jnp.concatenate([held[-2][1][p], held[-1][1][p]], axis=0) for p in range(2))
+            put_split(high, low, (len(held) - 2) * z.half, 2 * z.half, pair)
+
+    staged_dft(z.outer, -1, load, store, mid)
+    out = dot3(high[...], low[...], high_m, low_m)
+    for i, (k, _) in enumerate(held):
+        for part in range(2):
+            keep[part * z.outer + k] = out[i * z.half : (i + 1) * z.half, part * LANES : (part + 1) * LANES]
+
+
 def start_kernel(z, *refs):
     sources, refs = refs[:8], refs[8:]
-    tabs, pack, refs = refs[0], refs[1], refs[2:]
-    keeps, sends, refs = refs[: z.chunks], refs[z.chunks : 2 * z.chunks], refs[2 * z.chunks :]
+    tabs, pack, keep, refs = refs[0], refs[1], refs[2], refs[3:]
     held, (lines, mid, high, low, sems) = refs[:8], refs[8:]
+    bit = lax.axis_index("sub") & 1
+    rows = pl.ds(pl.multiple_of(bit * z.half, z.half), z.half)
+    sources = [*sources[:4], sources[4].at[:, rows], *sources[5:]]
     copies = [
         pltpu.make_async_copy(source, place, sems.at[i])
         for i, (source, place) in enumerate(zip(sources, held))
@@ -312,29 +325,26 @@
         copy.wait()
     prepare(z, *held[:4], tabs, pack, lines)
     image, twiddle, high_m, low_m = held[4:]
-    copies[4].wait()
-    copies[5].wait()
+    for copy in copies[4:]:
+        copy.wait()
 
     def load(q):
         cut = slice(q * LANES, (q + 1) * LANES)
         return image[0, :, cut], image[1, :, cut]
 
-    def store(k, value):
-        c, s = twiddle[0, k : k + 1, :], twiddle[1, k : k + 1, :]
-        value = (value[0] * c - value[1] * s, value[0] * s + value[1] * c)
-        put_split(high, low, k * z.rows, z.rows, value)
-
-    staged_dft(z.outer, -1, load, store, mid)
+    forward(z, load, keep, mid, high, low, high_m[...], low_m[...], twiddle)
+
+
+def join_kernel(z, image, twiddle, high_m, low_m, kept, near, far, wide_high, wide_low, keep, send, spectrum, mid, high, low):
     bit = lax.axis_index("sub") & 1
-    size = z.group * z.rows
-    copies[6].wait()
-    copies[7].wait()
-    for g in range(z.chunks):
-        cut = slice(g * size, (g + 1) * size)
-        out = dot3(high[cut], low[cut], high_m[...], low_m[...])
-        for i in range(z.group):
-            block = out[i * z.rows : (i + 1) * z.rows]
-            put_halves(keeps[g], sends[g], bit, z.group, i, block, z.half)
+    rows = pl.ds(pl.multiple_of(bit * z.half, z.half), z.half)
+
+    def load(q):
+        cut = slice(q * LANES, (q + 1) * LANES)
+        return image[0, rows, cut], image[1, rows, cut]
+
+    forward(z, load, spectrum, mid, high, low, high_m[...], low_m[...], twiddle)
+    level_kernel(z, 0, 0, 0, z.outer, kept, spectrum, near, far, wide_high, wide_low, keep, send, high, low)
 
 
 def rotated(value, near, far, k):
@@ -346,24 +356,24 @@
     return value[0] * rr - value[1] * ri, value[0] * ri + value[1] * rr
 
 
-def blended(z, level, chunk, keep, arrived, near, far, wide_high, wide_low, high, low):
+def blended(z, level, chunk, stride, keep, arrived, near, far, wide_high, wide_low, high, low):
     close = near[level, 0], near[level, 1]
     steps = far[level, 0], far[level, 1]
     for i in range(z.group):
-        value = tuple(
-            jnp.concatenate([keep[part * z.group + i], arrived[part * z.group + i]], axis=0)
-            for part in range(2)
-        )
+        spots = [part * z.group + i for part in range(2)]
+        if stride:
+            spots = [part * stride + chunk * z.group + i for part in range(2)]
+        value = tuple(jnp.concatenate([keep[spot], arrived[spot]], axis=0) for spot in spots)
         value = rotated(value, close, steps, chunk * z.group + i)
         put_split(high, low, i * z.rows, z.rows, value)
     return dot3(wide_high[level], wide_low[level], high[...], low[...])
 
 
-def level_kernel(z, level, chunk, riding, kept, arrived, *refs):
+def level_kernel(z, level, chunk, riding, stride, kept, arrived, *refs):
     packs, refs = refs[:riding], refs[riding:]
     near, far, wide_high, wide_low, keep, send, high, low = refs
     bit = lax.axis_index("sub") >> (level + 1) & 1
-    out = blended(z, level, chunk, kept, arrived, near, far, wide_high, wide_low, high, low)
+    out = blended(z, level, chunk, stride, kept, arrived, near, far, wide_high, wide_low, high, low)
     for i in range(z.group):
         put_halves(keep, send, bit, z.group, i, out[i * z.rows : (i + 1) * z.rows], z.half)
     if riding:
@@ -375,7 +385,7 @@
     z, chunk, kept, arrived, near, far, wide_high, wide_low, last_near, last_far,
     high_m, low_m, twiddle, back, high, low,
 ):
-    out = blended(z, z.last - 1, chunk, kept, arrived, near, far, wide_high, wide_low, high, low)
+    out = blended(z, z.last - 1, chunk, 0, kept, arrived, near, far, wide_high, wide_low, high, low)
     close = last_near[0], last_near[1]
     steps = last_far[0], last_far[1]
     for i in range(z.group):
@@ -410,12 +420,11 @@
     gather_back(z, backs, store, mid)
 
 
-def deal_kernel(z, per_block, riding, *refs):
-    pairs = z.sub_count // 2
+def deal_kernel(z, per_block, messages, riding, *refs):
     lines = 2 * per_block * z.rows
     backs, refs = refs[: z.chunks], refs[z.chunks :]
     sent, arrived, refs = refs[0], refs[1], refs[2:]
-    outs, (records, mid, whole) = refs[:pairs], refs[pairs:]
+    outs, (records, mid, whole) = refs[: len(messages)], refs[len(messages) :]
 
     def store(q, value):
         for part in range(2):
@@ -424,13 +433,13 @@
 
     gather_back(z, backs, store, mid)
     me = lax.axis_index("sub")
-    for k in range(pairs):
-        for side in range(2):
-            outs[k][side * lines : (side + 1) * lines] = whole[me ^ (2 * k + side)]
+    for out, aways in zip(outs, messages):
+        for i, away in enumerate(aways):
+            out[i * lines : (i + 1) * lines] = whole[me ^ away]
     known = (sent[2 * z.group :] + arrived[2 * z.group :]).reshape(-1, LANES)
     records[...] = known
-    if riding:
-        outs[1][2 * lines :] = known
+    if riding is not None:
+        outs[riding][2 * lines :] = known
 
 
 def stack_kernel(lines, count, *refs):
@@ -443,8 +452,13 @@
         refs[-1][count * lines :] = known
 
 
-def turn_kernel(z, per_block, places, *refs):
-    blend_high, blend_low, out_ref = refs[-3:]
+def turn_kernel(z, per_block, places, first, adding, *refs):
+    scratch = refs[len(refs) - 2 * adding :]
+    refs = refs[: len(refs) - 2 * adding]
+    blend_high, blend_low, *partial, out_ref = refs[len(refs) - 3 - adding :]
+    size = len(places) * z.rows
+    cut = slice(first, first + size)
+    copies = []
     for part in range(2 * per_block):
         line = []
         for array, at in places:
@@ -453,12 +467,24 @@
         line = jnp.concatenate(line, axis=0).T
         high = line.astype(bf16)
         low = (line - high.astype(f32)).astype(bf16)
-        a, cut = part // per_block, part % per_block
-        out_ref[a, cut * LANES : (cut + 1) * LANES, :] = dot3(high, low, blend_high[...], blend_low[...])
+        total = dot3(high, low, blend_high[cut], blend_low[cut])
+        at = (part // per_block, slice(part % per_block * LANES, (part % per_block + 1) * LANES))
+        if adding:
+            ready, sems = scratch
+            ready[at] = total + partial[0][at]
+            copies.append(pltpu.make_async_copy(ready.at[at], out_ref.at[at], sems.at[part]))
+            copies[-1].start()
+        else:
+            out_ref[at] = total
+    for copy in copies:
+        copy.wait()
 
 
 def pair_order(pairs):
-    return [*range(pairs // 2, pairs), *range(1, pairs // 2)]
+    order = []
+    for k in [*range(pairs // 2, pairs), *range(1, pairs // 2)]:
+        order += [(2 * k,), (2 * k + 1,)] if k in [] else [(2 * k, 2 * k + 1)]
+    return order
 
 
 def body(sub_images, shift_table, phase_table, offset_table, weight_table):
@@ -473,23 +499,28 @@
     halves = [pltpu.VMEM((size, 2 * LANES), bf16)] * 2
     slab = shape((2 * z.group, z.half, LANES), f32)
 
-    sources = [shift_table, phase_table, offset_table, weight_table, sub_images]
-    sources += [jnp.asarray(table) for table in (lane_twiddle(outer, -1), *lane_matrix(-1, 1.0))]
+    def swap(send, level):
+        return swapped(send, "sub", level)
+
+    raw = swap(sub_images, 0)
+    constants = [jnp.asarray(table) for table in (lane_twiddle(outer, -1), *lane_matrix(-1, 1.0))]
+    sources = [shift_table, phase_table, offset_table, weight_table, sub_images, *constants]
     sources = [pltpu.with_memory_space_constraint(source, pltpu.HBM) for source in sources]
-    tabs, pack, *parts = call(
+    spectra = shape((2 * outer, z.half, LANES), f32)
+    small = pltpu.VMEM((2, outer, z.half, LANES), f32)
+    places = [source.shape for source in sources]
+    places[4] = (2, z.half, range_bins)
+    tabs, pack, kept = call(
         functools.partial(start_kernel, z),
-        [shape((rows, z.pages * LANES), f32), shape((rows + z.blocks * z.record, LANES), f32)]
-        + [slab] * (2 * z.chunks),
+        [shape((rows, z.pages * LANES), f32), shape((rows + z.blocks * z.record, LANES), f32), spectra],
         sources,
-        [pltpu.VMEM(source.shape, source.dtype) for source in sources]
-        + [pltpu.VMEM((z.pages * LANES, LANES), f32), mid]
-        + [pltpu.VMEM((outer * rows, 2 * LANES), bf16)] * 2
+        [pltpu.VMEM(place, source.dtype) for place, source in zip(places, sources)]
+        + [pltpu.VMEM((z.pages * LANES, LANES), f32), small]
+        + [pltpu.VMEM((outer * z.half, 2 * LANES), bf16)] * 2
         + [pltpu.SemaphoreType.DMA((len(sources),))],
-        flops * z.chunks,
+        flops * z.chunks // 2,
         space=pltpu.HBM,
     )
-    keeps, sends = parts[: z.chunks], parts[z.chunks :]
-    arrived = [swapped(send, "sub", 0) for send in sends]
     tables = call(
         functools.partial(tables_kernel, z),
         [shape((z.last, 2, rows, LANES), f32)] * 2 + [shape((z.last, size, size), bf16)] * 2,
@@ -497,26 +528,33 @@
         [],
         1 << 20,
     )
+    keep, send, spectrum = call(
+        functools.partial(join_kernel, z),
+        [slab, slab, spectra],
+        [raw, *constants, kept, *tables],
+        [small] + [pltpu.VMEM((outer * z.half, 2 * LANES), bf16)] * 2,
+        flops * (1 + z.chunks // 2),
+    )
+    keeps, sends = [kept] * z.chunks, [None] * z.chunks
+    arrived = [spectrum] * z.chunks
+    keeps[0], sends[0], arrived[0] = keep, send, swap(send, 1)
+
     other = swapped(pack, "sub", z.last)
     tail = z.blocks * z.record
     longer = shape((2 * z.group + tail // z.half, z.half, LANES), f32)
     for level in range(z.last - 1):
-        for chunk in range(z.chunks):
+        for chunk in range(0 if level else 1, z.chunks):
             rides = level == z.last - 2 and chunk == z.chunks - 1
             keeps[chunk], sends[chunk] = call(
-                functools.partial(level_kernel, z, level, chunk, 2 * rides),
+                functools.partial(level_kernel, z, level, chunk, 2 * rides, 0 if level else z.outer),
                 [slab, longer if rides else slab],
                 [keeps[chunk], arrived[chunk]] + [pack, other] * rides + list(tables),
                 halves,
                 flops,
             )
-            arrived[chunk] = swapped(sends[chunk], "sub", level + 1)
+            arrived[chunk] = swap(sends[chunk], level + 1)
     last_tables = call(
-        functools.partial(last_tables_kernel, z),
-        [shape((2, rows, LANES), f32)] * 2,
-        [pack, other],
-        [],
-        1 << 16,
+        functools.partial(last_tables_kernel, z), [shape((2, rows, LANES), f32)] * 2, [pack, other], [], 1 << 16
     )
     way_back = [*lane_matrix(1, 1.0 / range_bins), lane_twiddle(outer, 1)]
     backs = [
@@ -533,11 +571,7 @@
     beams = sub_count * rows
     if block % LANES or beams > MXU or sub_count < 8:
         (children,) = call(
-            functools.partial(ranges_kernel, z),
-            [shape((outer, 2, rows, LANES), f32)],
-            backs,
-            [mid],
-            flops,
+            functools.partial(ranges_kernel, z), [shape((outer, 2, rows, LANES), f32)], backs, [mid], flops
         )
         known = (sends[-1] + arrived[-1])[2 * z.group :].reshape(-1, LANES)
         for level in range(z.last - 1):
@@ -548,48 +582,67 @@
     pairs = sub_count // 2
     lines = 2 * per_block * rows
     riding = z.last > 2
-    *messages, known = call(
-        functools.partial(deal_kernel, z, per_block, riding),
-        [shape((2 * lines + (tail if riding and k == 1 else 0), LANES), f32) for k in range(pairs)]
+    messages = [(0, 1)] + [away for away in pair_order(pairs)]
+    *dealt, known = call(
+        functools.partial(deal_kernel, z, per_block, messages, messages.index((2, 3)) if riding else None),
+        [
+            shape((len(aways) * lines + tail * (riding and aways == (2, 3)), LANES), f32)
+            for aways in messages
+        ]
         + [shape((tail, LANES), f32)],
         [*backs, sends[-1], arrived[-1]],
         [mid, pltpu.VMEM((sub_count, lines, LANES), f32)],
         flops,
     )
-    arrays = [messages[0]] + [None] * (pairs - 1)
-    for k in pair_order(pairs):
-        route = [(i, i ^ (2 * k)) for i in range(sub_count)]
-        arrays[k] = lax.ppermute(messages[k], "sub", route)
-    places = {2 * k: (k, 0) for k in range(pairs)}
-    cuts = [list(range(pairs // 2)), list(range(pairs // 2, pairs))]
-    crossing = []
-    for cut in cuts:
-        records = [] if crossing else [known] + [arrays[1]] * riding
+    got, places = {}, {}
+    for aways, message in zip(messages, dealt):
+        if aways[0] > 0:
+            route = [(i, i ^ aways[0]) for i in range(sub_count)]
+            message = lax.ppermute(message, "sub", route)
+        got[aways] = message
+        places[aways[0]] = (message, 0)
+    early = [k for k in range(pairs) if k // 2 % 2 == 0]
+    late = [k for k in range(pairs) if k // 2 % 2]
+    blend, partial = None, []
+    for cut in (early, late):
+        swaps = [(2 * k, 2 * k + 1) for k in cut if (2 * k, 2 * k + 1) in got]
+        records = [known] + [got[2, 3]] * riding if cut is early else []
         (both,) = call(
-            functools.partial(stack_kernel, lines, len(cut)),
-            [shape((len(cut) * lines + tail * bool(records), LANES), f32)],
-            [arrays[k] for k in cut] + records,
+            functools.partial(stack_kernel, lines, len(swaps)),
+            [shape((len(swaps) * lines + tail * bool(records), LANES), f32)],
+            [got[pair] for pair in swaps] + records,
             [],
             1,
         )
-        places.update({2 * k + 1: (len(arrays), i * lines) for i, k in enumerate(cut)})
-        crossing.append(both)
-        arrays.append(swapped(both, "sub", 0))
-    blend = call(
-        functools.partial(last_blend_kernel, z),
-        [shape((beams, beams), bf16)] * 2,
-        [crossing[0], arrays[pairs]],
-        [],
-        1 << 18,
-    )
-    (turned,) = call(
-        functools.partial(turn_kernel, z, per_block, [places[away] for away in range(sub_count)]),
-        [shape((2, block, beams), f32)],
-        [*arrays, *blend],
-        [],
-        flops,
-    )
-    return turned
+        crossed = swapped(both, "sub", 0)
+        places.update({pair[1]: (crossed, i * lines) for i, pair in enumerate(swaps)})
+        order = [2 * k + side for k in cut for side in range(2)]
+        if cut is early:
+            blend = call(
+                functools.partial(last_blend_kernel, z, order + [2 * k + side for k in late for side in range(2)]),
+                [shape((beams, beams), bf16)] * 2,
+                [both, crossed],
+                [],
+                1 << 18,
+            )
+        arrays = []
+        spots = []
+        for away in order:
+            array, at = places[away]
+            index = [i for i, other in enumerate(arrays) if other is array]
+            if not index:
+                index = [len(arrays)]
+                arrays.append(array)
+            spots.append((index[0], at))
+        partial = call(
+            functools.partial(turn_kernel, z, per_block, spots, 0 if cut is early else len(order) * rows, len(partial)),
+            [shape((2, block, beams), f32)],
+            [*arrays, *blend, *partial],
+            [pltpu.VMEM((2, block, beams), f32), pltpu.SemaphoreType.DMA((2 * per_block,))] * len(partial),
+            flops,
+            out_space=pltpu.HBM if partial else pltpu.VMEM,
+        )
+    return partial[0]
 
 
 def wide_turn(z, block, children, known):
@@ -629,6 +682,4 @@
         P(None, "sub", None, None, None),
     )
 
-    return jax.shard_map(
-        body, mesh=mesh, in_specs=placed, out_specs=P(None, ("img", "sub"), None), check_vma=False
-    )
+    return jax.shard_map(body, mesh=mesh, in_specs=placed, out_specs=P(None, ("img", "sub"), None), check_vma=False)

time: 42.2 us -> 41.2 us (0.976)
  waiting for transfers between devices: 12.5 us -> 9.1 us
  starting transfers between devices: 22 us -> 24 us
    ppermute x7, waiting for transfers between devices: 6.95 us -> 4.74 us  [body(): message = lax.ppermute(message, 'sub', route)]
    ppermute x7, starting transfers between devices: 11.5 us -> 13.6 us  [body(): message = lax.ppermute(message, 'sub', route)]
    ppermute x9 -> x8, waiting for transfers between devices: 5.5 us -> 4.35 us  [swapped(): return lax.ppermute(block, axis, route)]
    pallas_call x14 -> x15, Pallas kernels: 7.41 us -> 7.72 us  [call(): pl.pallas_call(kernel, out_shape=outs, in_specs=[pl.BlockSpec(memory_spac...]
    ppermute x9 -> x8, starting transfers between devices: 10.5 us -> 10.4 us  [swapped(): return lax.ppermute(block, axis, route)]
  transfers between devices with their start and end apart: 16 -> 15, of which waited for: 7 -> 6; matrix products, arithmetic and copies ran while one was open for 0% -> 0% of each run, Pallas kernels for 8% -> 12%
where the time goes in v1:
time: 41.2 us; the launch traced here: 41 us
  starting transfers between devices  24 us (58%)
  waiting for transfers between devices  9.1 us (22%)
  Pallas kernels  7.72 us (19%)
    ppermute x7, starting transfers between devices, body(): message = lax.ppermute(message, 'sub', route)  13.6 us
    ppermute x8, starting transfers between devices, swapped(): return lax.ppermute(block, axis, route)  10.4 us
    pallas_call x15, Pallas kernels, call(): pl.pallas_call(kernel, out_shape=outs, in_specs=[pl.BlockSpec(memory_spac...  7.72 us
    ppermute x7, waiting for transfers between devices, body(): message = lax.ppermute(message, 'sub', route)  4.74 us
    ppermute x8, waiting for transfers between devices, swapped(): return lax.ppermute(block, axis, route)  4.35 us
  transfers between devices with their start and end apart: 15, of which 6 were waited for; matrix products, arithmetic and copies ran while one was open for 0% of the time, Pallas kernels for 12%

profile of v1, /device:TPU:0, one launch (start us, length us, event | category | flops | bytes accessed | tf_op | source)
XLA Modules:
  0.0 41.0 jit_solution(7186163168416955409)
XLA Ops:
  0.0 0.0 copy-start.2
  0.0 0.0 copy-start.3
  0.0 0.5 %collective-permute-start = (f32[2,16,4096]{2,1,0:T(8,128)}, f32[2,16,4096]{2,1,0:T(8,128)S(1)}, u32[]{:S(2)}, u32[]{:S(2)}) collective-permute-start(f32[2,16,4096]{2,1,0:T(8,128)} %refs_4_.1), channel_id=1, source_target_pairs={{0,1},{1,0},{2,3},{3,2},{4,5},{5,4},{6,7},{7,6},{8,9},{9,8},{10,11... | collective-permute-start | bytes 1572872 | tf_op jit(solution)/shard_map/ppermute | solution.py:28
  0.5 0.0 copy-start.4
  0.5 1.5 %shard_map.109 = (f32[16,128]{1,0:T(8,128)S(1)}, f32[48,128]{1,0:T(8,128)S(1)}, f32[64,8,128]{2,1,0:T(8,128)S(1)}) custom-call(s32[4,1,2,8]{3,2,1,0:T(2,128)} %refs_0_.1, f32[4,1,2,8]{3,2,1,0:T(2,128)} %refs_1_.1, s32[4,1,2,16]{3,2,1,0:T(2,128)} %refs_2_.1, f32[4,1,2,4,16]{4,3,2,1,0:T(4,128)} %refs_3_.1, f32[2,16,4096]{2,1,0:T(8,128)} %refs_4_.1, ...), custom_call_target="tpu_custom_call" | custom-call | flops 100663296 | bytes 1117184 | tf_op jit(solution)/shard_map/pallas_call | solution.py:34
  2.1 0.4 shard_map.110
  2.5 0.0 collective-permute-done.image
  2.5 0.0 copy-done.2
  2.5 0.0 copy-done.3
  2.5 0.0 copy-done.4
  2.5 0.8 %shard_map.111 = (f32[32,8,128]{2,1,0:T(8,128)S(1)}, f32[32,8,128]{2,1,0:T(8,128)S(1)}, f32[64,8,128]{2,1,0:T(8,128)S(1)}) custom-call(f32[2,16,4096]{2,1,0:T(8,128)S(1)} %collective-permute-done.image, f32[2,32,128]{2,1,0:T(8,128)S(1)} %copy-done.4, bf16[256,256]{1,0:T(8,128)(2,1)S(1)} %copy-done.2, bf16[256,256]{1,0:T(8,128)(2,1)S(1)} %copy-done.3, ...), custom_call_target="tpu_custom_call" | custom-call | flops 201326592 | bytes 2490368 | tf_op jit(solution)/shard_map/pallas_call | solution.py:34
  3.3 2.7 %collective-permute-start.1 = (f32[32,8,128]{2,1,0:T(8,128)S(1)}, f32[32,8,128]{2,1,0:T(8,128)S(1)}, u32[]{:S(2)}, u32[]{:S(2)}) collective-permute-start(f32[32,8,128]{2,1,0:T(8,128)S(1)} %get-tuple-element.41), channel_id=1, source_target_pairs={{0,2},{2,0},{1,3},{3,1},{4,6},{6,4},{5,7},{7,5},{8,10},{10,8},{9,1... | collective-permute-start | bytes 393224 | tf_op jit(solution)/shard_map/ppermute | solution.py:28
  6.0 0.4 %shard_map.115 = (f32[32,8,128]{2,1,0:T(8,128)S(1)}, f32[32,8,128]{2,1,0:T(8,128)S(1)}) custom-call(f32[64,8,128]{2,1,0:T(8,128)S(1)} %get-tuple-element.34.kept, f32[64,8,128]{2,1,0:T(8,128)S(1)} %get-tuple-element.47.arrived, f32[3,2,16,128]{3,2,1,0:T(8,128)S(1)} %get-tuple-element.36.near.refs_0_.refs_2_, ...), custom_call_target="tpu_custom_call" | custom-call | flops 100663296 | bytes 1671168 | tf_op jit(solution)/shard_map/pallas_call | solution.py:34
  6.4 0.1 collective-permute-start.4
  6.5 3.1 %collective-permute-start.3 = (f32[48,128]{1,0:T(8,128)S(1)}, f32[48,128]{1,0:T(8,128)S(1)}, u32[]{:S(2)}, u32[]{:S(2)}) collective-permute-start(f32[48,128]{1,0:T(8,128)S(1)} %get-tuple-element.44.pack.refs_0_), channel_id=1, source_target_pairs={{0,8},{8,0},{1,9},{9,1},{2,10},{10,2},{3,11},{11,3},{4,12},{12,4},... | collective-permute-start | bytes 73736 | tf_op jit(solution)/shard_map/ppermute | solution.py:28
  9.6 0.7 %collective-permute-done.1.arrived = f32[32,8,128]{2,1,0:T(8,128)S(1)} collective-permute-done((f32[32,8,128]{2,1,0:T(8,128)S(1)}, f32[32,8,128]{2,1,0:T(8,128)S(1)}, u32[]{:S(2)}, u32[]{:S(2)}) %collective-permute-start.1) | collective-permute-done | bytes 131104 | tf_op jit(solution)/shard_map/ppermute | solution.py:28
  10.3 0.4 %shard_map.112 = (f32[32,8,128]{2,1,0:T(8,128)S(1)}, f32[32,8,128]{2,1,0:T(8,128)S(1)}) custom-call(f32[32,8,128]{2,1,0:T(8,128)S(1)} %get-tuple-element.40.kept, f32[32,8,128]{2,1,0:T(8,128)S(1)} %collective-permute-done.1.arrived, f32[3,2,16,128]{3,2,1,0:T(8,128)S(1)} %get-tuple-element.36.near.refs_0_.refs_2_, ...), custom_call_target="tpu_custom_call" | custom-call | flops 100663296 | bytes 1409024 | tf_op jit(solution)/shard_map/pallas_call | solution.py:34
  10.8 2.1 %collective-permute-start.2 = (f32[32,8,128]{2,1,0:T(8,128)S(1)}, f32[32,8,128]{2,1,0:T(8,128)S(1)}, u32[]{:S(2)}, u32[]{:S(2)}) collective-permute-start(f32[32,8,128]{2,1,0:T(8,128)S(1)} %get-tuple-element.43), channel_id=1, source_target_pairs={{0,4},{4,0},{1,5},{5,1},{2,6},{6,2},{3,7},{7,3},{8,12},{12,8},{9,1... | collective-permute-start | bytes 393224 | tf_op jit(solution)/shard_map/ppermute | solution.py:28
  12.9 0.0 collective-permute-done.3.other.refs_1_
  12.9 0.0 collective-permute-done.4.arrived
  12.9 0.0 copy-start
  12.9 0.0 copy-start.1
  12.9 0.4 %shard_map.116 = (f32[32,8,128]{2,1,0:T(8,128)S(1)}, f32[36,8,128]{2,1,0:T(8,128)S(1)}) custom-call(f32[32,8,128]{2,1,0:T(8,128)S(1)} %get-tuple-element.48.kept, f32[32,8,128]{2,1,0:T(8,128)S(1)} %collective-permute-done.4.arrived, f32[48,128]{1,0:T(8,128)S(1)} %get-tuple-element.44.pack.refs_0_, f32[48,128]{1,0:T(8,128)S(1)} %collective-permute-done.3.other.refs_1_, ...), custom_call_target="tpu_custom_call" | custom-call | flops 100663296 | bytes 1474560 | tf_op jit(solution)/shard_map/pallas_call | solution.py:34
  13.4 0.0 copy-start.5
  13.4 1.8 %collective-permute-start.5 = (f32[36,8,128]{2,1,0:T(8,128)S(1)}, f32[36,8,128]{2,1,0:T(8,128)S(1)}, u32[]{:S(2)}, u32[]{:S(2)}) collective-permute-start(f32[36,8,128]{2,1,0:T(8,128)S(1)} %get-tuple-element.51.refs_2_), channel_id=1, source_target_pairs={{0,4},{4,0},{1,5},{5,1},{2,6},{6,2},{3,7},{7,3},{8,12},{12,8},{9,1... | collective-permute-start | bytes 442376 | tf_op jit(solution)/shard_map/ppermute | solution.py:28
  15.2 0.2 shard_map.113
  15.4 0.6 %collective-permute-done.2.arrived = f32[32,8,128]{2,1,0:T(8,128)S(1)} collective-permute-done((f32[32,8,128]{2,1,0:T(8,128)S(1)}, f32[32,8,128]{2,1,0:T(8,128)S(1)}, u32[]{:S(2)}, u32[]{:S(2)}) %collective-permute-start.2) | collective-permute-done | bytes 131104 | tf_op jit(solution)/shard_map/ppermute | solution.py:28
  16.0 0.0 copy-done
  16.0 0.0 copy-done.1
  16.0 0.0 copy-done.5
  16.0 0.8 %shard_map.114.refs_0_ = f32[2,16,16,128]{3,2,1,0:T(8,128)S(1)} custom-call(f32[32,8,128]{2,1,0:T(8,128)S(1)} %get-tuple-element.42.kept, f32[32,8,128]{2,1,0:T(8,128)S(1)} %collective-permute-done.2.arrived, f32[3,2,16,128]{3,2,1,0:T(8,128)S(1)} %get-tuple-element.36.near.refs_0_.refs_2_, f32[3,2,16,128]{3,2,1,0:T(8,128)S(1)} %get-tuple-element.37.far.refs_1_.refs_3_, ...), custom_call_target="tpu_custom_call" | custom-call | flops 201326592 | bytes 1736704 | tf_op jit(solution)/shard_map/pallas_call | solution.py:34
  16.8 2.2 %collective-permute-done.5.arrived.refs_3_ = f32[36,8,128]{2,1,0:T(8,128)S(1)} collective-permute-done((f32[36,8,128]{2,1,0:T(8,128)S(1)}, f32[36,8,128]{2,1,0:T(8,128)S(1)}, u32[]{:S(2)}, u32[]{:S(2)}) %collective-permute-start.5) | collective-permute-done | bytes 147488 | tf_op jit(solution)/shard_map/ppermute | solution.py:28
  19.0 0.8 %shard_map.117.refs_1_ = f32[2,16,16,128]{3,2,1,0:T(8,128)S(1)} custom-call(f32[32,8,128]{2,1,0:T(8,128)S(1)} %get-tuple-element.50.kept, f32[36,8,128]{2,1,0:T(8,128)S(1)} %collective-permute-done.5.arrived.refs_3_, f32[3,2,16,128]{3,2,1,0:T(8,128)S(1)} %get-tuple-element.36.near.refs_0_.refs_2_, ...), custom_call_target="tpu_custom_call" | custom-call | flops 201326592 | bytes 1753088 | tf_op jit(solution)/shard_map/pallas_call | solution.py:34
  19.8 0.2 shard_map.118
  20.0 3.1 %collective-permute-start.12 = (f32[128,128]{1,0:T(8,128)S(1)}, f32[128,128]{1,0:T(8,128)S(1)}, u32[]{:S(2)}, u32[]{:S(2)}) collective-permute-start(f32[128,128]{1,0:T(8,128)S(1)} %get-tuple-element.58), channel_id=1, source_target_pairs={{0,8},{1,9},{2,10},{3,11},{4,12},{5,13},{6,14},{7,15},{8,0},{9,1},... | collective-permute-start | bytes 196616 | tf_op jit(solution)/shard_map/ppermute | solution.py:601
  23.1 1.3 %collective-permute-start.13 = (f32[128,128]{1,0:T(8,128)S(1)}, f32[128,128]{1,0:T(8,128)S(1)}, u32[]{:S(2)}, u32[]{:S(2)}) collective-permute-start(f32[128,128]{1,0:T(8,128)S(1)} %get-tuple-element.59), channel_id=1, source_target_pairs={{0,10},{1,11},{2,8},{3,9},{4,14},{5,15},{6,12},{7,13},{8,2},{9,3},... | collective-permute-start | bytes 196616 | tf_op jit(solution)/shard_map/ppermute | solution.py:601
  24.4 0.3 collective-permute-start.11
  24.7 1.8 %collective-permute-start.6 = (f32[128,128]{1,0:T(8,128)S(1)}, f32[128,128]{1,0:T(8,128)S(1)}, u32[]{:S(2)}, u32[]{:S(2)}) collective-permute-start(f32[128,128]{1,0:T(8,128)S(1)} %get-tuple-element.52), channel_id=1, source_target_pairs={{0,4},{1,5},{2,6},{3,7},{4,0},{5,1},{6,2},{7,3},{8,12},{9,13},{10,... | collective-permute-start | bytes 196616 | tf_op jit(solution)/shard_map/ppermute | solution.py:601
  26.5 1.4 %collective-permute-start.7 = (f32[128,128]{1,0:T(8,128)S(1)}, f32[128,128]{1,0:T(8,128)S(1)}, u32[]{:S(2)}, u32[]{:S(2)}) collective-permute-start(f32[128,128]{1,0:T(8,128)S(1)} %get-tuple-element.53), channel_id=1, source_target_pairs={{0,6},{1,7},{2,4},{3,5},{4,2},{5,3},{6,0},{7,1},{8,14},{9,15},{10,... | collective-permute-start | bytes 196616 | tf_op jit(solution)/shard_map/ppermute | solution.py:601
  27.9 0.0 collective-permute-done.12.refs_2_.refs_3_
  27.9 3.6 %collective-permute-start.8 = (f32[128,128]{1,0:T(8,128)S(1)}, f32[128,128]{1,0:T(8,128)S(1)}, u32[]{:S(2)}, u32[]{:S(2)}) collective-permute-start(f32[128,128]{1,0:T(8,128)S(1)} %get-tuple-element.54), channel_id=1, source_target_pairs={{0,12},{1,13},{2,14},{3,15},{4,8},{5,9},{6,10},{7,11},{8,4},{9,5},... | collective-permute-start | bytes 196616 | tf_op jit(solution)/shard_map/ppermute | solution.py:601
  31.5 0.0 collective-permute-done.13.refs_3_.refs_4_
  31.5 2.1 %collective-permute-start.9 = (f32[128,128]{1,0:T(8,128)S(1)}, f32[128,128]{1,0:T(8,128)S(1)}, u32[]{:S(2)}, u32[]{:S(2)}) collective-permute-start(f32[128,128]{1,0:T(8,128)S(1)} %get-tuple-element.55), channel_id=1, source_target_pairs={{0,14},{1,15},{2,12},{3,13},{4,10},{5,11},{6,8},{7,9},{8,6},{9,7},... | collective-permute-start | bytes 196616 | tf_op jit(solution)/shard_map/ppermute | solution.py:601
  33.6 0.0 collective-permute-done.11.refs_1_.refs_5_.refs_2_
  33.6 0.1 collective-permute-start.14
  33.7 0.0 collective-permute-done.6.refs_0_
  33.7 0.0 collective-permute-done.7.refs_1_.refs_2_
  33.7 0.8 %collective-permute-done.8.refs_2_.refs_3_ = f32[128,128]{1,0:T(8,128)S(1)} collective-permute-done((f32[128,128]{1,0:T(8,128)S(1)}, f32[128,128]{1,0:T(8,128)S(1)}, u32[]{:S(2)}, u32[]{:S(2)}) %collective-permute-start.8) | collective-permute-done | bytes 65568 | tf_op jit(solution)/shard_map/ppermute | solution.py:601
  34.5 3.9 %collective-permute-done.9.refs_3_.refs_4_ = f32[128,128]{1,0:T(8,128)S(1)} collective-permute-done((f32[128,128]{1,0:T(8,128)S(1)}, f32[128,128]{1,0:T(8,128)S(1)}, u32[]{:S(2)}, u32[]{:S(2)}) %collective-permute-start.9) | collective-permute-done | bytes 65568 | tf_op jit(solution)/shard_map/ppermute | solution.py:601
  38.5 0.1 collective-permute-start.10
  38.6 0.0 collective-permute-done.14.theirs.refs_1_
  38.6 0.1 shard_map.121
  38.7 0.4 shard_map.122.refs_7_
  39.1 0.8 %collective-permute-done.10.refs_1_ = f32[256,128]{1,0:T(8,128)S(1)} collective-permute-done((f32[256,128]{1,0:T(8,128)S(1)}, f32[256,128]{1,0:T(8,128)S(1)}, u32[]{:S(2)}, u32[]{:S(2)}) %collective-permute-start.10) | collective-permute-done | bytes 131104 | tf_op jit(solution)/shard_map/ppermute | solution.py:28
  39.9 1.1 %shard_map.123 = f32[2,256,256]{2,1,0:T(8,128)} custom-call(f32[128,128]{1,0:T(8,128)S(1)} %collective-permute-done.6.refs_0_, f32[256,128]{1,0:T(8,128)S(1)} %collective-permute-done.10.refs_1_, f32[128,128]{1,0:T(8,128)S(1)} %collective-permute-done.7.refs_1_.refs_2_, f32[128,128]{1,0:T(8,128)S(1)} %collective-permute-done.8.refs_2_.refs_3_, ...), custom_call_target="tpu_custom_call" | custom-call | flops 100663296 | bytes 1703936 | tf_op jit(solution)/shard_map/pallas_call | solution.py:34
  (2 shorter events, 0.0 us)
Async XLA Ops:
  0.0 2.5 %copy-start.2 = (bf16[256,256]{1,0:T(8,128)(2,1)S(1)}, bf16[256,256]{1,0:T(8,128)(2,1)}, u32[]{:S(2)}) copy-start(bf16[256,256]{1,0:T(8,128)(2,1)} %constant.13.clone.refs_6_.high_m) | copy-start | bytes 393220
  0.0 2.5 %copy-start.3 = (bf16[256,256]{1,0:T(8,128)(2,1)S(1)}, bf16[256,256]{1,0:T(8,128)(2,1)}, u32[]{:S(2)}) copy-start(bf16[256,256]{1,0:T(8,128)(2,1)} %constant.14.clone.refs_7_.low_m) | copy-start | bytes 393220
  0.0 2.5 %collective-permute-start = (f32[2,16,4096]{2,1,0:T(8,128)}, f32[2,16,4096]{2,1,0:T(8,128)S(1)}, u32[]{:S(2)}, u32[]{:S(2)}) collective-permute-start(f32[2,16,4096]{2,1,0:T(8,128)} %refs_4_.1), channel_id=1, source_target_pairs={{0,1},{1,0},{2,3},{3,2},{4,5},{5,4},{6,7},{7,6},{8,9},{9,8},{10,11... | collective-permute-start | bytes 1572872 | tf_op jit(solution)/shard_map/ppermute | solution.py:28
  0.5 2.0 %copy-start.4 = (f32[2,32,128]{2,1,0:T(8,128)S(1)}, f32[2,32,128]{2,1,0:T(8,128)}, u32[]{:S(2)}) copy-start(f32[2,32,128]{2,1,0:T(8,128)} %constant.12.clone.refs_5_.twiddle) | copy-start | bytes 98308
  3.3 7.0 %collective-permute-start.1 = (f32[32,8,128]{2,1,0:T(8,128)S(1)}, f32[32,8,128]{2,1,0:T(8,128)S(1)}, u32[]{:S(2)}, u32[]{:S(2)}) collective-permute-start(f32[32,8,128]{2,1,0:T(8,128)S(1)} %get-tuple-element.41), channel_id=1, source_target_pairs={{0,2},{2,0},{1,3},{3,1},{4,6},{6,4},{5,7},{7,5},{8,10},{10,8},{9,1... | collective-permute-start | bytes 393224 | tf_op jit(solution)/shard_map/ppermute | solution.py:28
  6.4 6.5 %collective-permute-start.4 = (f32[32,8,128]{2,1,0:T(8,128)S(1)}, f32[32,8,128]{2,1,0:T(8,128)S(1)}, u32[]{:S(2)}, u32[]{:S(2)}) collective-permute-start(f32[32,8,128]{2,1,0:T(8,128)S(1)} %get-tuple-element.49), channel_id=1, source_target_pairs={{0,2},{2,0},{1,3},{3,1},{4,6},{6,4},{5,7},{7,5},{8,10},{10,8},{9,1... | collective-permute-start | bytes 393224 | tf_op jit(solution)/shard_map/ppermute | solution.py:28
  6.5 6.4 %collective-permute-start.3 = (f32[48,128]{1,0:T(8,128)S(1)}, f32[48,128]{1,0:T(8,128)S(1)}, u32[]{:S(2)}, u32[]{:S(2)}) collective-permute-start(f32[48,128]{1,0:T(8,128)S(1)} %get-tuple-element.44.pack.refs_0_), channel_id=1, source_target_pairs={{0,8},{8,0},{1,9},{9,1},{2,10},{10,2},{3,11},{11,3},{4,12},{12,4},... | collective-permute-start | bytes 73736 | tf_op jit(solution)/shard_map/ppermute | solution.py:28
  10.8 5.2 %collective-permute-start.2 = (f32[32,8,128]{2,1,0:T(8,128)S(1)}, f32[32,8,128]{2,1,0:T(8,128)S(1)}, u32[]{:S(2)}, u32[]{:S(2)}) collective-permute-start(f32[32,8,128]{2,1,0:T(8,128)S(1)} %get-tuple-element.43), channel_id=1, source_target_pairs={{0,4},{4,0},{1,5},{5,1},{2,6},{6,2},{3,7},{7,3},{8,12},{12,8},{9,1... | collective-permute-start | bytes 393224 | tf_op jit(solution)/shard_map/ppermute | solution.py:28
  12.9 3.1 %copy-start = (bf16[256,256]{1,0:T(8,128)(2,1)S(1)}, bf16[256,256]{1,0:T(8,128)(2,1)}, u32[]{:S(2)}) copy-start(bf16[256,256]{1,0:T(8,128)(2,1)} %constant.15.clone.high_m) | copy-start | bytes 393220
  12.9 3.1 %copy-start.1 = (bf16[256,256]{1,0:T(8,128)(2,1)S(1)}, bf16[256,256]{1,0:T(8,128)(2,1)}, u32[]{:S(2)}) copy-start(bf16[256,256]{1,0:T(8,128)(2,1)} %constant.16.clone.low_m) | copy-start | bytes 393220
  13.4 2.6 %copy-start.5 = (f32[2,32,128]{2,1,0:T(8,128)S(1)}, f32[2,32,128]{2,1,0:T(8,128)}, u32[]{:S(2)}) copy-start(f32[2,32,128]{2,1,0:T(8,128)} %constant.17.clone.twiddle) | copy-start | bytes 98308
  13.4 5.6 %collective-permute-start.5 = (f32[36,8,128]{2,1,0:T(8,128)S(1)}, f32[36,8,128]{2,1,0:T(8,128)S(1)}, u32[]{:S(2)}, u32[]{:S(2)}) collective-permute-start(f32[36,8,128]{2,1,0:T(8,128)S(1)} %get-tuple-element.51.refs_2_), channel_id=1, source_target_pairs={{0,4},{4,0},{1,5},{5,1},{2,6},{6,2},{3,7},{7,3},{8,12},{12,8},{9,1... | collective-permute-start | bytes 442376 | tf_op jit(solution)/shard_map/ppermute | solution.py:28
  20.0 7.9 %collective-permute-start.12 = (f32[128,128]{1,0:T(8,128)S(1)}, f32[128,128]{1,0:T(8,128)S(1)}, u32[]{:S(2)}, u32[]{:S(2)}) collective-permute-start(f32[128,128]{1,0:T(8,128)S(1)} %get-tuple-element.58), channel_id=1, source_target_pairs={{0,8},{1,9},{2,10},{3,11},{4,12},{5,13},{6,14},{7,15},{8,0},{9,1},... | collective-permute-start | bytes 196616 | tf_op jit(solution)/shard_map/ppermute | solution.py:601
  23.1 8.4 %collective-permute-start.13 = (f32[128,128]{1,0:T(8,128)S(1)}, f32[128,128]{1,0:T(8,128)S(1)}, u32[]{:S(2)}, u32[]{:S(2)}) collective-permute-start(f32[128,128]{1,0:T(8,128)S(1)} %get-tuple-element.59), channel_id=1, source_target_pairs={{0,10},{1,11},{2,8},{3,9},{4,14},{5,15},{6,12},{7,13},{8,2},{9,3},... | collective-permute-start | bytes 196616 | tf_op jit(solution)/shard_map/ppermute | solution.py:601
  24.4 9.2 %collective-permute-start.11 = (f32[160,128]{1,0:T(8,128)S(1)}, f32[160,128]{1,0:T(8,128)S(1)}, u32[]{:S(2)}, u32[]{:S(2)}) collective-permute-start(f32[160,128]{1,0:T(8,128)S(1)} %get-tuple-element.57), channel_id=1, source_target_pairs={{0,2},{1,3},{2,0},{3,1},{4,6},{5,7},{6,4},{7,5},{8,10},{9,11},{10,... | collective-permute-start | bytes 245768 | tf_op jit(solution)/shard_map/ppermute | solution.py:601
  24.7 9.1 %collective-permute-start.6 = (f32[128,128]{1,0:T(8,128)S(1)}, f32[128,128]{1,0:T(8,128)S(1)}, u32[]{:S(2)}, u32[]{:S(2)}) collective-permute-start(f32[128,128]{1,0:T(8,128)S(1)} %get-tuple-element.52), channel_id=1, source_target_pairs={{0,4},{1,5},{2,6},{3,7},{4,0},{5,1},{6,2},{7,3},{8,12},{9,13},{10,... | collective-permute-start | bytes 196616 | tf_op jit(solution)/shard_map/ppermute | solution.py:601
  26.5 7.2 %collective-permute-start.7 = (f32[128,128]{1,0:T(8,128)S(1)}, f32[128,128]{1,0:T(8,128)S(1)}, u32[]{:S(2)}, u32[]{:S(2)}) collective-permute-start(f32[128,128]{1,0:T(8,128)S(1)} %get-tuple-element.53), channel_id=1, source_target_pairs={{0,6},{1,7},{2,4},{3,5},{4,2},{5,3},{6,0},{7,1},{8,14},{9,15},{10,... | collective-permute-start | bytes 196616 | tf_op jit(solution)/shard_map/ppermute | solution.py:601
  27.9 6.6 %collective-permute-start.8 = (f32[128,128]{1,0:T(8,128)S(1)}, f32[128,128]{1,0:T(8,128)S(1)}, u32[]{:S(2)}, u32[]{:S(2)}) collective-permute-start(f32[128,128]{1,0:T(8,128)S(1)} %get-tuple-element.54), channel_id=1, source_target_pairs={{0,12},{1,13},{2,14},{3,15},{4,8},{5,9},{6,10},{7,11},{8,4},{9,5},... | collective-permute-start | bytes 196616 | tf_op jit(solution)/shard_map/ppermute | solution.py:601
  31.5 7.0 %collective-permute-start.9 = (f32[128,128]{1,0:T(8,128)S(1)}, f32[128,128]{1,0:T(8,128)S(1)}, u32[]{:S(2)}, u32[]{:S(2)}) collective-permute-start(f32[128,128]{1,0:T(8,128)S(1)} %get-tuple-element.55), channel_id=1, source_target_pairs={{0,14},{1,15},{2,12},{3,13},{4,10},{5,11},{6,8},{7,9},{8,6},{9,7},... | collective-permute-start | bytes 196616 | tf_op jit(solution)/shard_map/ppermute | solution.py:601
  33.6 4.9 %collective-permute-start.14 = (f32[288,128]{1,0:T(8,128)S(1)}, f32[288,128]{1,0:T(8,128)S(1)}, u32[]{:S(2)}, u32[]{:S(2)}) collective-permute-start(f32[288,128]{1,0:T(8,128)S(1)} %shard_map.120.ours), channel_id=1, source_target_pairs={{0,1},{1,0},{2,3},{3,2},{4,5},{5,4},{6,7},{7,6},{8,9},{9,8},{10,11... | collective-permute-start | bytes 442376 | tf_op jit(solution)/shard_map/ppermute | solution.py:28
  38.5 1.4 %collective-permute-start.10 = (f32[256,128]{1,0:T(8,128)S(1)}, f32[256,128]{1,0:T(8,128)S(1)}, u32[]{:S(2)}, u32[]{:S(2)}) collective-permute-start(f32[256,128]{1,0:T(8,128)S(1)} %shard_map.119), channel_id=1, source_target_pairs={{0,1},{1,0},{2,3},{3,2},{4,5},{5,4},{6,7},{7,6},{8,9},{9,8},{10,11... | collective-permute-start | bytes 393224 | tf_op jit(solution)/shard_map/ppermute | solution.py:28

commit v2 on v1

--- a/solution.py
+++ b/solution.py
@@ -452,6 +452,14 @@
         refs[-1][count * lines :] = known
 
 
+def merge_kernel(lines, *refs):
+    count = len(refs) // 2
+    mine, theirs, outs = refs[:count], refs[count], refs[count + 1 :]
+    for i in range(count):
+        outs[i][:lines] = mine[i][...]
+        outs[i][lines:] = theirs[i * lines : (i + 1) * lines]
+
+
 def turn_kernel(z, per_block, places, first, adding, *refs):
     scratch = refs[len(refs) - 2 * adding :]
     refs = refs[: len(refs) - 2 * adding]
@@ -480,11 +488,12 @@
         copy.wait()
 
 
+def groups(pairs):
+    return [k for k in range(pairs) if k // 2 % 2 == 0], [k for k in range(pairs) if k // 2 % 2]
+
+
 def pair_order(pairs):
-    order = []
-    for k in [*range(pairs // 2, pairs), *range(1, pairs // 2)]:
-        order += [(2 * k,), (2 * k + 1,)] if k in [] else [(2 * k, 2 * k + 1)]
-    return order
+    return [*range(pairs // 2, pairs), *range(1, pairs // 2)]
 
 
 def body(sub_images, shift_table, phase_table, offset_table, weight_table):
@@ -554,7 +563,11 @@
             )
             arrived[chunk] = swap(sends[chunk], level + 1)
     last_tables = call(
-        functools.partial(last_tables_kernel, z), [shape((2, rows, LANES), f32)] * 2, [pack, other], [], 1 << 16
+        functools.partial(last_tables_kernel, z),
+        [shape((2, rows, LANES), f32)] * 2,
+        [pack, other],
+        [],
+        1 << 16,
     )
     way_back = [*lane_matrix(1, 1.0 / range_bins), lane_twiddle(outer, 1)]
     backs = [
@@ -571,7 +584,11 @@
     beams = sub_count * rows
     if block % LANES or beams > MXU or sub_count < 8:
         (children,) = call(
-            functools.partial(ranges_kernel, z), [shape((outer, 2, rows, LANES), f32)], backs, [mid], flops
+            functools.partial(ranges_kernel, z),
+            [shape((outer, 2, rows, LANES), f32)],
+            backs,
+            [mid],
+            flops,
         )
         known = (sends[-1] + arrived[-1])[2 * z.group :].reshape(-1, LANES)
         for level in range(z.last - 1):
@@ -582,7 +599,9 @@
     pairs = sub_count // 2
     lines = 2 * per_block * rows
     riding = z.last > 2
-    messages = [(0, 1)] + [away for away in pair_order(pairs)]
+    early, late = groups(pairs)
+    messages = [(2 * k, 2 * k + 1) for k in early] + [(2 * k,) for k in late]
+    messages.append(tuple(2 * k + 1 for k in late))
     *dealt, known = call(
         functools.partial(deal_kernel, z, per_block, messages, messages.index((2, 3)) if riding else None),
         [
@@ -594,55 +613,55 @@
         [mid, pltpu.VMEM((sub_count, lines, LANES), f32)],
         flops,
     )
-    got, places = {}, {}
-    for aways, message in zip(messages, dealt):
-        if aways[0] > 0:
-            route = [(i, i ^ aways[0]) for i in range(sub_count)]
-            message = lax.ppermute(message, "sub", route)
-        got[aways] = message
-        places[aways[0]] = (message, 0)
-    early = [k for k in range(pairs) if k // 2 % 2 == 0]
-    late = [k for k in range(pairs) if k // 2 % 2]
-    blend, partial = None, []
-    for cut in (early, late):
-        swaps = [(2 * k, 2 * k + 1) for k in cut if (2 * k, 2 * k + 1) in got]
-        records = [known] + [got[2, 3]] * riding if cut is early else []
-        (both,) = call(
-            functools.partial(stack_kernel, lines, len(swaps)),
-            [shape((len(swaps) * lines + tail * bool(records), LANES), f32)],
-            [got[pair] for pair in swaps] + records,
-            [],
-            1,
-        )
-        crossed = swapped(both, "sub", 0)
-        places.update({pair[1]: (crossed, i * lines) for i, pair in enumerate(swaps)})
-        order = [2 * k + side for k in cut for side in range(2)]
-        if cut is early:
-            blend = call(
-                functools.partial(last_blend_kernel, z, order + [2 * k + side for k in late for side in range(2)]),
-                [shape((beams, beams), bf16)] * 2,
-                [both, crossed],
-                [],
-                1 << 18,
-            )
-        arrays = []
-        spots = []
-        for away in order:
-            array, at = places[away]
-            index = [i for i, other in enumerate(arrays) if other is array]
-            if not index:
-                index = [len(arrays)]
-                arrays.append(array)
-            spots.append((index[0], at))
-        partial = call(
-            functools.partial(turn_kernel, z, per_block, spots, 0 if cut is early else len(order) * rows, len(partial)),
-            [shape((2, block, beams), f32)],
-            [*arrays, *blend, *partial],
-            [pltpu.VMEM((2, block, beams), f32), pltpu.SemaphoreType.DMA((2 * per_block,))] * len(partial),
-            flops,
-            out_space=pltpu.HBM if partial else pltpu.VMEM,
-        )
-    return partial[0]
+    theirs = swapped(dealt[-1], "sub", 0)
+    merged = call(
+        functools.partial(merge_kernel, lines),
+        [shape((2 * lines, LANES), f32)] * len(late),
+        [*dealt[len(early) : -1], theirs],
+        [],
+        1,
+    )
+    outgoing = dict(zip([*early, *late], [*dealt[: len(early)], *merged]))
+    got = {0: outgoing[0]}
+    for k in pair_order(pairs):
+        route = [(i, i ^ (2 * k)) for i in range(sub_count)]
+        got[k] = lax.ppermute(outgoing[k], "sub", route)
+    records = [known] + [got[1]] * riding
+    (both,) = call(
+        functools.partial(stack_kernel, lines, len(early)),
+        [shape((len(early) * lines + tail, LANES), f32)],
+        [got[k] for k in early] + records,
+        [],
+        1,
+    )
+    crossed = swapped(both, "sub", 0)
+    order = [2 * k + side for k in [*early, *late] for side in range(2)]
+    blend = call(
+        functools.partial(last_blend_kernel, z, order),
+        [shape((beams, beams), bf16)] * 2,
+        [both, crossed],
+        [],
+        1 << 18,
+    )
+    count = len(early)
+    spots = [spot for i in range(count) for spot in ((i, 0), (count, i * lines))]
+    partial = call(
+        functools.partial(turn_kernel, z, per_block, spots, 0, 0),
+        [shape((2, block, beams), f32)],
+        [got[k] for k in early] + [crossed, *blend],
+        [],
+        flops,
+    )
+    spots = [(i, side * lines) for i in range(len(late)) for side in range(2)]
+    (turned,) = call(
+        functools.partial(turn_kernel, z, per_block, spots, 2 * count * rows, 1),
+        [shape((2, block, beams), f32)],
+        [got[k] for k in late] + [*blend, *partial],
+        [pltpu.VMEM((2, block, beams), f32), pltpu.SemaphoreType.DMA((2 * per_block,))],
+        flops,
+        out_space=pltpu.HBM,
+    )
+    return turned
 
 
 def wide_turn(z, block, children, known):
@@ -682,4 +701,6 @@
         P(None, "sub", None, None, None),
     )
 
-    return jax.shard_map(body, mesh=mesh, in_specs=placed, out_specs=P(None, ("img", "sub"), None), check_vma=False)
+    return jax.shard_map(
+        body, mesh=mesh, in_specs=placed, out_specs=P(None, ("img", "sub"), None), check_vma=False
+    )

time: 41.2 us -> 44 us (1.068)
  waiting for transfers between devices: 9.1 us -> 14.2 us
  starting transfers between devices: 24 us -> 21.8 us
    ppermute x7, waiting for transfers between devices: 4.74 us -> 10.7 us  [body(): got[k] = lax.ppermute(outgoing[k], 'sub', route)]
    ppermute x7, starting transfers between devices: 13.6 us -> 11.4 us  [body(): got[k] = lax.ppermute(outgoing[k], 'sub', route)]
    ppermute x8, waiting for transfers between devices: 4.35 us -> 3.54 us  [swapped(): return lax.ppermute(block, axis, route)]
  transfers between devices with their start and end apart: 15 -> 15, of which waited for: 6 -> 9; matrix products, arithmetic and copies ran while one was open for 0% -> 0% of each run, Pallas kernels for 12% -> 11%
where the time goes in v2:
time: 44 us; the launch traced here: 43.9 us
  starting transfers between devices  21.8 us (50%)
  waiting for transfers between devices  14.2 us (32%)
  Pallas kernels  7.73 us (18%)
    ppermute x7, starting transfers between devices, body(): got[k] = lax.ppermute(outgoing[k], 'sub', route)  11.4 us
    ppermute x7, waiting for transfers between devices, body(): got[k] = lax.ppermute(outgoing[k], 'sub', route)  10.7 us
    ppermute x8, starting transfers between devices, swapped(): return lax.ppermute(block, axis, route)  10.3 us
    pallas_call x15, Pallas kernels, call(): pl.pallas_call(kernel, out_shape=outs, in_specs=[pl.BlockSpec(memory_spac...  7.73 us
    ppermute x8, waiting for transfers between devices, swapped(): return lax.ppermute(block, axis, route)  3.54 us
  transfers between devices with their start and end apart: 15, of which 9 were waited for; matrix products, arithmetic and copies ran while one was open for 0% of the time, Pallas kernels for 11%

profile of v2, /device:TPU:0, one launch (start us, length us, event | category | flops | bytes accessed | tf_op | source)
XLA Modules:
  0.0 43.9 jit_solution(17209401651798008246)
XLA Ops:
  0.0 0.0 copy-start.2
  0.0 0.0 copy-start.3
  0.0 0.5 %collective-permute-start = (f32[2,16,4096]{2,1,0:T(8,128)}, f32[2,16,4096]{2,1,0:T(8,128)S(1)}, u32[]{:S(2)}, u32[]{:S(2)}) collective-permute-start(f32[2,16,4096]{2,1,0:T(8,128)} %refs_4_.1), channel_id=1, source_target_pairs={{0,1},{1,0},{2,3},{3,2},{4,5},{5,4},{6,7},{7,6},{8,9},{9,8},{10,11... | collective-permute-start | bytes 1572872 | tf_op jit(solution)/shard_map/ppermute | solution.py:28
  0.5 0.0 copy-start.4
  0.5 1.5 %shard_map.109 = (f32[16,128]{1,0:T(8,128)S(1)}, f32[48,128]{1,0:T(8,128)S(1)}, f32[64,8,128]{2,1,0:T(8,128)S(1)}) custom-call(s32[4,1,2,8]{3,2,1,0:T(2,128)} %refs_0_.1, f32[4,1,2,8]{3,2,1,0:T(2,128)} %refs_1_.1, s32[4,1,2,16]{3,2,1,0:T(2,128)} %refs_2_.1, f32[4,1,2,4,16]{4,3,2,1,0:T(4,128)} %refs_3_.1, f32[2,16,4096]{2,1,0:T(8,128)} %refs_4_.1, ...), custom_call_target="tpu_custom_call" | custom-call | flops 100663296 | bytes 1117184 | tf_op jit(solution)/shard_map/pallas_call | solution.py:34
  2.1 0.4 shard_map.110
  2.5 0.0 collective-permute-done.image
  2.5 0.0 copy-done.2
  2.5 0.0 copy-done.3
  2.5 0.0 copy-done.4
  2.5 0.8 %shard_map.111 = (f32[32,8,128]{2,1,0:T(8,128)S(1)}, f32[32,8,128]{2,1,0:T(8,128)S(1)}, f32[64,8,128]{2,1,0:T(8,128)S(1)}) custom-call(f32[2,16,4096]{2,1,0:T(8,128)S(1)} %collective-permute-done.image, f32[2,32,128]{2,1,0:T(8,128)S(1)} %copy-done.4, bf16[256,256]{1,0:T(8,128)(2,1)S(1)} %copy-done.2, bf16[256,256]{1,0:T(8,128)(2,1)S(1)} %copy-done.3, ...), custom_call_target="tpu_custom_call" | custom-call | flops 201326592 | bytes 2490368 | tf_op jit(solution)/shard_map/pallas_call | solution.py:34
  3.3 2.7 %collective-permute-start.1 = (f32[32,8,128]{2,1,0:T(8,128)S(1)}, f32[32,8,128]{2,1,0:T(8,128)S(1)}, u32[]{:S(2)}, u32[]{:S(2)}) collective-permute-start(f32[32,8,128]{2,1,0:T(8,128)S(1)} %get-tuple-element.46), channel_id=1, source_target_pairs={{0,2},{2,0},{1,3},{3,1},{4,6},{6,4},{5,7},{7,5},{8,10},{10,8},{9,1... | collective-permute-start | bytes 393224 | tf_op jit(solution)/shard_map/ppermute | solution.py:28
  6.0 0.4 %shard_map.115 = (f32[32,8,128]{2,1,0:T(8,128)S(1)}, f32[32,8,128]{2,1,0:T(8,128)S(1)}) custom-call(f32[64,8,128]{2,1,0:T(8,128)S(1)} %get-tuple-element.39.kept, f32[64,8,128]{2,1,0:T(8,128)S(1)} %get-tuple-element.52.arrived, f32[3,2,16,128]{3,2,1,0:T(8,128)S(1)} %get-tuple-element.41.near.refs_0_.refs_2_, ...), custom_call_target="tpu_custom_call" | custom-call | flops 100663296 | bytes 1671168 | tf_op jit(solution)/shard_map/pallas_call | solution.py:34
  6.4 0.1 collective-permute-start.4
  6.5 3.1 %collective-permute-start.3 = (f32[48,128]{1,0:T(8,128)S(1)}, f32[48,128]{1,0:T(8,128)S(1)}, u32[]{:S(2)}, u32[]{:S(2)}) collective-permute-start(f32[48,128]{1,0:T(8,128)S(1)} %get-tuple-element.49.pack.refs_0_), channel_id=1, source_target_pairs={{0,8},{8,0},{1,9},{9,1},{2,10},{10,2},{3,11},{11,3},{4,12},{12,4},... | collective-permute-start | bytes 73736 | tf_op jit(solution)/shard_map/ppermute | solution.py:28
  9.6 0.7 %collective-permute-done.1.arrived = f32[32,8,128]{2,1,0:T(8,128)S(1)} collective-permute-done((f32[32,8,128]{2,1,0:T(8,128)S(1)}, f32[32,8,128]{2,1,0:T(8,128)S(1)}, u32[]{:S(2)}, u32[]{:S(2)}) %collective-permute-start.1) | collective-permute-done | bytes 131104 | tf_op jit(solution)/shard_map/ppermute | solution.py:28
  10.3 0.4 %shard_map.112 = (f32[32,8,128]{2,1,0:T(8,128)S(1)}, f32[32,8,128]{2,1,0:T(8,128)S(1)}) custom-call(f32[32,8,128]{2,1,0:T(8,128)S(1)} %get-tuple-element.45.kept, f32[32,8,128]{2,1,0:T(8,128)S(1)} %collective-permute-done.1.arrived, f32[3,2,16,128]{3,2,1,0:T(8,128)S(1)} %get-tuple-element.41.near.refs_0_.refs_2_, ...), custom_call_target="tpu_custom_call" | custom-call | flops 100663296 | bytes 1409024 | tf_op jit(solution)/shard_map/pallas_call | solution.py:34
  10.8 2.1 %collective-permute-start.2 = (f32[32,8,128]{2,1,0:T(8,128)S(1)}, f32[32,8,128]{2,1,0:T(8,128)S(1)}, u32[]{:S(2)}, u32[]{:S(2)}) collective-permute-start(f32[32,8,128]{2,1,0:T(8,128)S(1)} %get-tuple-element.48), channel_id=1, source_target_pairs={{0,4},{4,0},{1,5},{5,1},{2,6},{6,2},{3,7},{7,3},{8,12},{12,8},{9,1... | collective-permute-start | bytes 393224 | tf_op jit(solution)/shard_map/ppermute | solution.py:28
  12.9 0.0 collective-permute-done.3.other.refs_1_
  12.9 0.0 collective-permute-done.4.arrived
  12.9 0.0 copy-start
  12.9 0.0 copy-start.1
  12.9 0.4 %shard_map.116 = (f32[32,8,128]{2,1,0:T(8,128)S(1)}, f32[36,8,128]{2,1,0:T(8,128)S(1)}) custom-call(f32[32,8,128]{2,1,0:T(8,128)S(1)} %get-tuple-element.53.kept, f32[32,8,128]{2,1,0:T(8,128)S(1)} %collective-permute-done.4.arrived, f32[48,128]{1,0:T(8,128)S(1)} %get-tuple-element.49.pack.refs_0_, f32[48,128]{1,0:T(8,128)S(1)} %collective-permute-done.3.other.refs_1_, ...), custom_call_target="tpu_custom_call" | custom-call | flops 100663296 | bytes 1474560 | tf_op jit(solution)/shard_map/pallas_call | solution.py:34
  13.4 0.0 copy-start.5
  13.4 1.8 %collective-permute-start.5 = (f32[36,8,128]{2,1,0:T(8,128)S(1)}, f32[36,8,128]{2,1,0:T(8,128)S(1)}, u32[]{:S(2)}, u32[]{:S(2)}) collective-permute-start(f32[36,8,128]{2,1,0:T(8,128)S(1)} %get-tuple-element.56.refs_2_), channel_id=1, source_target_pairs={{0,4},{4,0},{1,5},{5,1},{2,6},{6,2},{3,7},{7,3},{8,12},{12,8},{9,1... | collective-permute-start | bytes 442376 | tf_op jit(solution)/shard_map/ppermute | solution.py:28
  15.2 0.2 shard_map.113
  15.4 0.6 %collective-permute-done.2.arrived = f32[32,8,128]{2,1,0:T(8,128)S(1)} collective-permute-done((f32[32,8,128]{2,1,0:T(8,128)S(1)}, f32[32,8,128]{2,1,0:T(8,128)S(1)}, u32[]{:S(2)}, u32[]{:S(2)}) %collective-permute-start.2) | collective-permute-done | bytes 131104 | tf_op jit(solution)/shard_map/ppermute | solution.py:28
  16.0 0.0 copy-done
  16.0 0.0 copy-done.1
  16.0 0.0 copy-done.5
  16.0 0.8 %shard_map.114.refs_0_ = f32[2,16,16,128]{3,2,1,0:T(8,128)S(1)} custom-call(f32[32,8,128]{2,1,0:T(8,128)S(1)} %get-tuple-element.47.kept, f32[32,8,128]{2,1,0:T(8,128)S(1)} %collective-permute-done.2.arrived, f32[3,2,16,128]{3,2,1,0:T(8,128)S(1)} %get-tuple-element.41.near.refs_0_.refs_2_, f32[3,2,16,128]{3,2,1,0:T(8,128)S(1)} %get-tuple-element.42.far.refs_1_.refs_3_, ...), custom_call_target="tpu_custom_call" | custom-call | flops 201326592 | bytes 1736704 | tf_op jit(solution)/shard_map/pallas_call | solution.py:34
  16.8 2.2 %collective-permute-done.5.arrived.refs_3_ = f32[36,8,128]{2,1,0:T(8,128)S(1)} collective-permute-done((f32[36,8,128]{2,1,0:T(8,128)S(1)}, f32[36,8,128]{2,1,0:T(8,128)S(1)}, u32[]{:S(2)}, u32[]{:S(2)}) %collective-permute-start.5) | collective-permute-done | bytes 147488 | tf_op jit(solution)/shard_map/ppermute | solution.py:28
  19.0 0.8 %shard_map.117.refs_1_ = f32[2,16,16,128]{3,2,1,0:T(8,128)S(1)} custom-call(f32[32,8,128]{2,1,0:T(8,128)S(1)} %get-tuple-element.55.kept, f32[36,8,128]{2,1,0:T(8,128)S(1)} %collective-permute-done.5.arrived.refs_3_, f32[3,2,16,128]{3,2,1,0:T(8,128)S(1)} %get-tuple-element.41.near.refs_0_.refs_2_, ...), custom_call_target="tpu_custom_call" | custom-call | flops 201326592 | bytes 1753088 | tf_op jit(solution)/shard_map/pallas_call | solution.py:34
  19.8 0.2 shard_map.118
  20.0 2.0 %collective-permute-start.11 = (f32[160,128]{1,0:T(8,128)S(1)}, f32[160,128]{1,0:T(8,128)S(1)}, u32[]{:S(2)}, u32[]{:S(2)}) collective-permute-start(f32[160,128]{1,0:T(8,128)S(1)} %get-tuple-element.67), channel_id=1, source_target_pairs={{0,2},{1,3},{2,0},{3,1},{4,6},{5,7},{6,4},{7,5},{8,10},{9,11},{10,... | collective-permute-start | bytes 245768 | tf_op jit(solution)/shard_map/ppermute | solution.py:628
  22.0 2.6 %collective-permute-start.12 = (f32[128,128]{1,0:T(8,128)S(1)}, f32[128,128]{1,0:T(8,128)S(1)}, u32[]{:S(2)}, u32[]{:S(2)}) collective-permute-start(f32[128,128]{1,0:T(8,128)S(1)} %get-tuple-element.68), channel_id=1, source_target_pairs={{0,8},{1,9},{2,10},{3,11},{4,12},{5,13},{6,14},{7,15},{8,0},{9,1},... | collective-permute-start | bytes 196616 | tf_op jit(solution)/shard_map/ppermute | solution.py:628
  24.6 0.0 collective-permute-start.13
  24.6 0.0 collective-permute-start.6
  24.6 4.4 %collective-permute-done.12.refs_2_ = f32[128,128]{1,0:T(8,128)S(1)} collective-permute-done((f32[128,128]{1,0:T(8,128)S(1)}, f32[128,128]{1,0:T(8,128)S(1)}, u32[]{:S(2)}, u32[]{:S(2)}) %collective-permute-start.12) | collective-permute-done | bytes 65568 | tf_op jit(solution)/shard_map/ppermute | solution.py:628
  29.0 1.7 %collective-permute-done.13.refs_3_ = f32[128,128]{1,0:T(8,128)S(1)} collective-permute-done((f32[128,128]{1,0:T(8,128)S(1)}, f32[128,128]{1,0:T(8,128)S(1)}, u32[]{:S(2)}, u32[]{:S(2)}) %collective-permute-start.13) | collective-permute-done | bytes 65568 | tf_op jit(solution)/shard_map/ppermute | solution.py:628
  30.7 0.0 collective-permute-done.11.refs_1_.refs_5_
  30.7 0.1 collective-permute-start.14
  30.8 0.0 collective-permute-done.6.refs_4_
  30.8 3.9 %collective-permute-start.10 = (f32[128,128]{1,0:T(8,128)S(1)}, f32[128,128]{1,0:T(8,128)S(1)}, u32[]{:S(2)}, u32[]{:S(2)}) collective-permute-start(f32[128,128]{1,0:T(8,128)S(1)} %get-tuple-element.65), channel_id=1, source_target_pairs={{0,14},{1,15},{2,12},{3,13},{4,10},{5,11},{6,8},{7,9},{8,6},{9,7},... | collective-permute-start | bytes 196616 | tf_op jit(solution)/shard_map/ppermute | solution.py:628
  34.7 0.0 collective-permute-start.7
  34.7 2.0 %collective-permute-start.8 = (f32[128,128]{1,0:T(8,128)S(1)}, f32[128,128]{1,0:T(8,128)S(1)}, u32[]{:S(2)}, u32[]{:S(2)}) collective-permute-start(f32[128,128]{1,0:T(8,128)S(1)} %get-tuple-element.63), channel_id=1, source_target_pairs={{0,6},{1,7},{2,4},{3,5},{4,2},{5,3},{6,0},{7,1},{8,14},{9,15},{10,... | collective-permute-start | bytes 196616 | tf_op jit(solution)/shard_map/ppermute | solution.py:628
  36.7 1.0 %collective-permute-start.9 = (f32[128,128]{1,0:T(8,128)S(1)}, f32[128,128]{1,0:T(8,128)S(1)}, u32[]{:S(2)}, u32[]{:S(2)}) collective-permute-start(f32[128,128]{1,0:T(8,128)S(1)} %get-tuple-element.64), channel_id=1, source_target_pairs={{0,12},{1,13},{2,14},{3,15},{4,8},{5,9},{6,10},{7,11},{8,4},{9,5},... | collective-permute-start | bytes 196616 | tf_op jit(solution)/shard_map/ppermute | solution.py:628
  37.6 0.0 collective-permute-done.14.theirs.refs_4_
  37.7 0.1 shard_map.121
  37.7 0.4 shard_map.122.refs_6_
  38.2 0.4 collective-permute-done.10.refs_3_
  38.6 1.1 %collective-permute-done.7.refs_0_ = f32[128,128]{1,0:T(8,128)S(1)} collective-permute-done((f32[128,128]{1,0:T(8,128)S(1)}, f32[128,128]{1,0:T(8,128)S(1)}, u32[]{:S(2)}, u32[]{:S(2)}) %collective-permute-start.7) | collective-permute-done | bytes 65568 | tf_op jit(solution)/shard_map/ppermute | solution.py:628
  39.7 1.3 %collective-permute-done.8.refs_1_ = f32[128,128]{1,0:T(8,128)S(1)} collective-permute-done((f32[128,128]{1,0:T(8,128)S(1)}, f32[128,128]{1,0:T(8,128)S(1)}, u32[]{:S(2)}, u32[]{:S(2)}) %collective-permute-start.8) | collective-permute-done | bytes 65568 | tf_op jit(solution)/shard_map/ppermute | solution.py:628
  41.0 1.8 %collective-permute-done.9.refs_2_ = f32[128,128]{1,0:T(8,128)S(1)} collective-permute-done((f32[128,128]{1,0:T(8,128)S(1)}, f32[128,128]{1,0:T(8,128)S(1)}, u32[]{:S(2)}, u32[]{:S(2)}) %collective-permute-start.9) | collective-permute-done | bytes 65568 | tf_op jit(solution)/shard_map/ppermute | solution.py:628
  42.8 1.1 %shard_map.123 = f32[2,256,256]{2,1,0:T(8,128)} custom-call(f32[128,128]{1,0:T(8,128)S(1)} %collective-permute-done.7.refs_0_, f32[128,128]{1,0:T(8,128)S(1)} %collective-permute-done.8.refs_1_, f32[128,128]{1,0:T(8,128)S(1)} %collective-permute-done.9.refs_2_, f32[128,128]{1,0:T(8,128)S(1)} %collective-permute-done.10.refs_3_, ...), custom_call_target="tpu_custom_call" | custom-call | flops 100663296 | bytes 1572864 | tf_op jit(solution)/shard_map/pallas_call | solution.py:34
  (2 shorter events, 0.0 us)
Async XLA Ops:
  0.0 2.5 %copy-start.2 = (bf16[256,256]{1,0:T(8,128)(2,1)S(1)}, bf16[256,256]{1,0:T(8,128)(2,1)}, u32[]{:S(2)}) copy-start(bf16[256,256]{1,0:T(8,128)(2,1)} %constant.13.clone.refs_6_.high_m) | copy-start | bytes 393220
  0.0 2.5 %copy-start.3 = (bf16[256,256]{1,0:T(8,128)(2,1)S(1)}, bf16[256,256]{1,0:T(8,128)(2,1)}, u32[]{:S(2)}) copy-start(bf16[256,256]{1,0:T(8,128)(2,1)} %constant.14.clone.refs_7_.low_m) | copy-start | bytes 393220
  0.0 2.5 %collective-permute-start = (f32[2,16,4096]{2,1,0:T(8,128)}, f32[2,16,4096]{2,1,0:T(8,128)S(1)}, u32[]{:S(2)}, u32[]{:S(2)}) collective-permute-start(f32[2,16,4096]{2,1,0:T(8,128)} %refs_4_.1), channel_id=1, source_target_pairs={{0,1},{1,0},{2,3},{3,2},{4,5},{5,4},{6,7},{7,6},{8,9},{9,8},{10,11... | collective-permute-start | bytes 1572872 | tf_op jit(solution)/shard_map/ppermute | solution.py:28
  0.5 2.0 %copy-start.4 = (f32[2,32,128]{2,1,0:T(8,128)S(1)}, f32[2,32,128]{2,1,0:T(8,128)}, u32[]{:S(2)}) copy-start(f32[2,32,128]{2,1,0:T(8,128)} %constant.12.clone.refs_5_.twiddle) | copy-start | bytes 98308
  3.3 7.0 %collective-permute-start.1 = (f32[32,8,128]{2,1,0:T(8,128)S(1)}, f32[32,8,128]{2,1,0:T(8,128)S(1)}, u32[]{:S(2)}, u32[]{:S(2)}) collective-permute-start(f32[32,8,128]{2,1,0:T(8,128)S(1)} %get-tuple-element.46), channel_id=1, source_target_pairs={{0,2},{2,0},{1,3},{3,1},{4,6},{6,4},{5,7},{7,5},{8,10},{10,8},{9,1... | collective-permute-start | bytes 393224 | tf_op jit(solution)/shard_map/ppermute | solution.py:28
  6.4 6.5 %collective-permute-start.4 = (f32[32,8,128]{2,1,0:T(8,128)S(1)}, f32[32,8,128]{2,1,0:T(8,128)S(1)}, u32[]{:S(2)}, u32[]{:S(2)}) collective-permute-start(f32[32,8,128]{2,1,0:T(8,128)S(1)} %get-tuple-element.54), channel_id=1, source_target_pairs={{0,2},{2,0},{1,3},{3,1},{4,6},{6,4},{5,7},{7,5},{8,10},{10,8},{9,1... | collective-permute-start | bytes 393224 | tf_op jit(solution)/shard_map/ppermute | solution.py:28
  6.5 6.4 %collective-permute-start.3 = (f32[48,128]{1,0:T(8,128)S(1)}, f32[48,128]{1,0:T(8,128)S(1)}, u32[]{:S(2)}, u32[]{:S(2)}) collective-permute-start(f32[48,128]{1,0:T(8,128)S(1)} %get-tuple-element.49.pack.refs_0_), channel_id=1, source_target_pairs={{0,8},{8,0},{1,9},{9,1},{2,10},{10,2},{3,11},{11,3},{4,12},{12,4},... | collective-permute-start | bytes 73736 | tf_op jit(solution)/shard_map/ppermute | solution.py:28
  10.8 5.2 %collective-permute-start.2 = (f32[32,8,128]{2,1,0:T(8,128)S(1)}, f32[32,8,128]{2,1,0:T(8,128)S(1)}, u32[]{:S(2)}, u32[]{:S(2)}) collective-permute-start(f32[32,8,128]{2,1,0:T(8,128)S(1)} %get-tuple-element.48), channel_id=1, source_target_pairs={{0,4},{4,0},{1,5},{5,1},{2,6},{6,2},{3,7},{7,3},{8,12},{12,8},{9,1... | collective-permute-start | bytes 393224 | tf_op jit(solution)/shard_map/ppermute | solution.py:28
  12.9 3.1 %copy-start = (bf16[256,256]{1,0:T(8,128)(2,1)S(1)}, bf16[256,256]{1,0:T(8,128)(2,1)}, u32[]{:S(2)}) copy-start(bf16[256,256]{1,0:T(8,128)(2,1)} %constant.15.clone.high_m) | copy-start | bytes 393220
  12.9 3.1 %copy-start.1 = (bf16[256,256]{1,0:T(8,128)(2,1)S(1)}, bf16[256,256]{1,0:T(8,128)(2,1)}, u32[]{:S(2)}) copy-start(bf16[256,256]{1,0:T(8,128)(2,1)} %constant.16.clone.low_m) | copy-start | bytes 393220
  13.4 2.6 %copy-start.5 = (f32[2,32,128]{2,1,0:T(8,128)S(1)}, f32[2,32,128]{2,1,0:T(8,128)}, u32[]{:S(2)}) copy-start(f32[2,32,128]{2,1,0:T(8,128)} %constant.17.clone.twiddle) | copy-start | bytes 98308
  13.4 5.6 %collective-permute-start.5 = (f32[36,8,128]{2,1,0:T(8,128)S(1)}, f32[36,8,128]{2,1,0:T(8,128)S(1)}, u32[]{:S(2)}, u32[]{:S(2)}) collective-permute-start(f32[36,8,128]{2,1,0:T(8,128)S(1)} %get-tuple-element.56.refs_2_), channel_id=1, source_target_pairs={{0,4},{4,0},{1,5},{5,1},{2,6},{6,2},{3,7},{7,3},{8,12},{12,8},{9,1... | collective-permute-start | bytes 442376 | tf_op jit(solution)/shard_map/ppermute | solution.py:28
  20.0 10.7 %collective-permute-start.11 = (f32[160,128]{1,0:T(8,128)S(1)}, f32[160,128]{1,0:T(8,128)S(1)}, u32[]{:S(2)}, u32[]{:S(2)}) collective-permute-start(f32[160,128]{1,0:T(8,128)S(1)} %get-tuple-element.67), channel_id=1, source_target_pairs={{0,2},{1,3},{2,0},{3,1},{4,6},{5,7},{6,4},{7,5},{8,10},{9,11},{10,... | collective-permute-start | bytes 245768 | tf_op jit(solution)/shard_map/ppermute | solution.py:628
  22.0 7.0 %collective-permute-start.12 = (f32[128,128]{1,0:T(8,128)S(1)}, f32[128,128]{1,0:T(8,128)S(1)}, u32[]{:S(2)}, u32[]{:S(2)}) collective-permute-start(f32[128,128]{1,0:T(8,128)S(1)} %get-tuple-element.68), channel_id=1, source_target_pairs={{0,8},{1,9},{2,10},{3,11},{4,12},{5,13},{6,14},{7,15},{8,0},{9,1},... | collective-permute-start | bytes 196616 | tf_op jit(solution)/shard_map/ppermute | solution.py:628
  24.6 6.1 %collective-permute-start.13 = (f32[128,128]{1,0:T(8,128)S(1)}, f32[128,128]{1,0:T(8,128)S(1)}, u32[]{:S(2)}, u32[]{:S(2)}) collective-permute-start(f32[128,128]{1,0:T(8,128)S(1)} %get-tuple-element.69), channel_id=1, source_target_pairs={{0,10},{1,11},{2,8},{3,9},{4,14},{5,15},{6,12},{7,13},{8,2},{9,3},... | collective-permute-start | bytes 196616 | tf_op jit(solution)/shard_map/ppermute | solution.py:628
  24.6 6.2 %collective-permute-start.6 = (f32[256,128]{1,0:T(8,128)S(1)}, f32[256,128]{1,0:T(8,128)S(1)}, u32[]{:S(2)}, u32[]{:S(2)}) collective-permute-start(f32[256,128]{1,0:T(8,128)S(1)} %get-tuple-element.61), channel_id=1, source_target_pairs={{0,1},{1,0},{2,3},{3,2},{4,5},{5,4},{6,7},{7,6},{8,9},{9,8},{10,11... | collective-permute-start | bytes 393224 | tf_op jit(solution)/shard_map/ppermute | solution.py:28
  30.7 6.9 %collective-permute-start.14 = (f32[288,128]{1,0:T(8,128)S(1)}, f32[288,128]{1,0:T(8,128)S(1)}, u32[]{:S(2)}, u32[]{:S(2)}) collective-permute-start(f32[288,128]{1,0:T(8,128)S(1)} %shard_map.120.ours), channel_id=1, source_target_pairs={{0,1},{1,0},{2,3},{3,2},{4,5},{5,4},{6,7},{7,6},{8,9},{9,8},{10,11... | collective-permute-start | bytes 442376 | tf_op jit(solution)/shard_map/ppermute | solution.py:28
  30.8 7.7 %collective-permute-start.10 = (f32[128,128]{1,0:T(8,128)S(1)}, f32[128,128]{1,0:T(8,128)S(1)}, u32[]{:S(2)}, u32[]{:S(2)}) collective-permute-start(f32[128,128]{1,0:T(8,128)S(1)} %get-tuple-element.65), channel_id=1, source_target_pairs={{0,14},{1,15},{2,12},{3,13},{4,10},{5,11},{6,8},{7,9},{8,6},{9,7},... | collective-permute-start | bytes 196616 | tf_op jit(solution)/shard_map/ppermute | solution.py:628
  34.7 5.0 %collective-permute-start.7 = (f32[128,128]{1,0:T(8,128)S(1)}, f32[128,128]{1,0:T(8,128)S(1)}, u32[]{:S(2)}, u32[]{:S(2)}) collective-permute-start(f32[128,128]{1,0:T(8,128)S(1)} %get-tuple-element.62), channel_id=1, source_target_pairs={{0,4},{1,5},{2,6},{3,7},{4,0},{5,1},{6,2},{7,3},{8,12},{9,13},{10,... | collective-permute-start | bytes 196616 | tf_op jit(solution)/shard_map/ppermute | solution.py:628
  34.7 6.3 %collective-permute-start.8 = (f32[128,128]{1,0:T(8,128)S(1)}, f32[128,128]{1,0:T(8,128)S(1)}, u32[]{:S(2)}, u32[]{:S(2)}) collective-permute-start(f32[128,128]{1,0:T(8,128)S(1)} %get-tuple-element.63), channel_id=1, source_target_pairs={{0,6},{1,7},{2,4},{3,5},{4,2},{5,3},{6,0},{7,1},{8,14},{9,15},{10,... | collective-permute-start | bytes 196616 | tf_op jit(solution)/shard_map/ppermute | solution.py:628
  36.7 6.1 %collective-permute-start.9 = (f32[128,128]{1,0:T(8,128)S(1)}, f32[128,128]{1,0:T(8,128)S(1)}, u32[]{:S(2)}, u32[]{:S(2)}) collective-permute-start(f32[128,128]{1,0:T(8,128)S(1)} %get-tuple-element.64), channel_id=1, source_target_pairs={{0,12},{1,13},{2,14},{3,15},{4,8},{5,9},{6,10},{7,11},{8,4},{9,5},... | collective-permute-start | bytes 196616 | tf_op jit(solution)/shard_map/ppermute | solution.py:628
